TPU v7x, 32 devices: a whole 2x2x4 slice. The times are simulated.
32 devices in a mesh: shard: 4 (over z), context: 4 (over y, x), tensor: 2 (over core).
Axes of the slice: x: 2, y: 2, z: 4, core: 2. Of those that a mesh axis runs over, the one named last changes fastest.
Arguments:
- tokens: bfloat16 [4, 1024, 1024], P('shard', 'context'), may hold values from -8 to 8
- segment_ids: int32 [4, 1024], P('shard'), may hold values from 0 to 3, never falling along the last dimension, each value on 1 to 512 neighbouring positions
- norm_gain: bfloat16 [1024], P('shard'), may hold values from 0.5 to 1.5
- in_proj: bfloat16 [1024, 2, 2048], P('shard', None, 'tensor'), may hold values from -0.1875 to 0.1875
- bc_proj: bfloat16 [1024, 256], P('shard'), may hold values from -0.1875 to 0.1875
- dt_proj: bfloat16 [1024, 32], P('shard', 'tensor'), may hold values from -0.1875 to 0.1875
- conv_weight: bfloat16 [4, 32, 64], P(None, 'tensor', 'shard'), may hold values from -3 to 3
- conv_bias: bfloat16 [32, 64], P('tensor', 'shard'), may hold values from -1.75 to 1.75
- bc_conv: bfloat16 [4, 256], P(None, 'shard'), may hold values from -3 to 3
- bc_bias: bfloat16 [256], P('shard'), may hold values from -1.75 to 1.75
- dt_bias: float32 [32], P('tensor'), may hold values from -4 to -1
- a_log: float32 [32], P('tensor'), may hold values from -9 to 0, as said below
- d_skip: float32 [32], P('tensor'), may hold values from 0.5 to 1.5
- out_gain: bfloat16 [32, 64], P('tensor', 'shard'), may hold values from 0.5 to 1.5
- out_proj: bfloat16 [2048, 1024], P('tensor', 'shard'), may hold values from -0.125 to 0.125
- cotangent: bfloat16 [4, 1024, 1024], P('shard', 'context'), may hold values from -8 to 8
Outputs:
- block_out: bfloat16 [4, 1024, 1024], P('shard', 'context', 'tensor')
- tokens_grad: float32 [4, 1024, 1024], P('shard', 'context')
- norm_gain_grad: float32 [1024], P('shard')
- in_proj_grad: float32 [1024, 2, 2048], P('shard', None, 'tensor')
- bc_proj_grad: float32 [1024, 256], P('shard')
- dt_proj_grad: float32 [1024, 32], P('shard', 'tensor')
- conv_weight_grad: float32 [4, 32, 64], P(None, 'tensor', 'shard')
- conv_bias_grad: float32 [32, 64], P('tensor', 'shard')
- bc_conv_grad: float32 [4, 256], P(None, 'shard')
- bc_bias_grad: float32 [256], P('shard')
- dt_bias_grad: float32 [32], P('tensor')
- a_log_grad: float32 [32], P('tensor')
- d_skip_grad: float32 [32], P('tensor')
- out_gain_grad: float32 [32, 64], P('tensor', 'shard')
- out_proj_grad: float32 [2048, 1024], P('tensor', 'shard')
Inputs may be any that keep to these rules, and one draw needn't show every extreme that they name: `segment_ids`: numbers never fall along a stream; each stream holds documents 0 to 3, each of 1 to 512 tokens, one exactly 512. `a_log`: one value a head.
All inputs are finite; a program needn't handle non-finite values.
Results may differ from a plain program's by a relative error of at most 0.012.
The roundings to bfloat16 on the way count: a program that leaves them out, or rounds other values in their place, can miss the bound.
Values may be sent and summed in bfloat16 or wider, within the bound.
No kernel may reach another device: no remote copies, remote signals or barrier semaphores. Data moves between devices by JAX's collectives and lax.ppermute only.
A program may use at most 128 MiB of HBM per device.

v0:
```python
import jax
import jax.numpy as jnp
from jax import lax
from jax.experimental import pallas as pl
from jax.experimental.pallas import tpu as pltpu
from jax.sharding import PartitionSpec as P

CONV = 4
SPAN = 128
PAD = 16
GAIN = 8
HEADP = 16
BCP = 24
RATE = 40
BCLO = 32
MISC = 128
eps = 1e-05
f32 = jnp.float32
bf16 = jnp.bfloat16


def mm(a, b, ca=1, cb=0):
    return lax.dot_general(a, b, (((ca,), (cb,)), ((), ())), preferred_element_type=f32)


def pieces(x, count):
    parts = []
    for _ in range(count):
        part = x.astype(bf16)
        parts.append(part)
        x = x - part.astype(f32)
    return parts


def mm3(a, b, ca=1, cb=0):
    ah, al = pieces(a, 2)
    bh, bl = pieces(b, 2)
    return mm(ah, bh, ca, cb) + (mm(al, bh, ca, cb) + mm(ah, bl, ca, cb))


def exact_left(ones, x, count, cb=0):
    return sum(mm(ones, part, 1, cb) for part in pieces(x, count))


def exact_right(x, ones, count, ca=1, cb=0):
    return sum(mm(part, ones, ca, cb) for part in pieces(x, count))


def iota(shape, dim):
    return lax.broadcasted_iota(jnp.int32, shape, dim)


def low(x, size):
    return lax.bitwise_and(x, jnp.int32(size - 1))


def high(x, size):
    return lax.shift_right_logical(x, jnp.int32(size.bit_length() - 1))


def sigmoid(x):
    return 1.0 / (1.0 + jnp.exp(-x))


def softplus(x):
    return jnp.maximum(x, 0.0) + jnp.log1p(jnp.exp(-jnp.abs(x)))


def spread_head(width, shards, channels, head):
    rows = width // shards
    part = head // shards
    used = (channels // head) * part
    r, c = iota((width, channels), 0), iota((width, channels), 1)
    s, q = high(r, rows), low(r, rows)
    hit = (c == high(q, part) * head + s * part + low(q, part)) & (q < used)
    return hit.astype(f32).astype(bf16)


def spread_bc(width, shards, channels):
    rows = width // shards
    part = channels // shards
    r, c = iota((width, channels), 0), iota((width, channels), 1)
    s, q = high(r, rows), low(r, rows)
    return ((c == s * part + q) & (q < part)).astype(f32).astype(bf16)


def spread_rate(width, shards, channels, head):
    rows = width // shards
    r, c = iota((width, channels), 0), iota((width, channels), 1)
    q = low(r, rows)
    return ((c == q * head) & (q < channels // head)).astype(f32).astype(bf16)


def block_ones(channels, head):
    r, c = iota((channels, channels), 0), iota((channels, channels), 1)
    return (high(r, head) == high(c, head)).astype(f32).astype(bf16)


def one_hot(rows, cols, row, col):
    return ((iota((rows, cols), 0) == row) & (iota((rows, cols), 1) == col)).astype(f32).astype(bf16)


def triangle(lower):
    r, c = iota((SPAN, SPAN), 0), iota((SPAN, SPAN), 1)
    hit = (r >= c) if lower else (r <= c)
    return hit.astype(f32).astype(bf16)


def local_decay(keep, a, at, head, h):
    diff = a[:, h * head : h * head + 1] - at[h * head : h * head + 1, :]
    return jnp.exp(jnp.where(keep, diff, -1e30))


def front_kernel(dims, *refs):
    shards, contexts, head, channels, state = dims
    it = iter(refs)
    idx = next(it)
    segr, masks, rates = next(it), next(it), next(it)
    own = next(it)
    mine = [next(it) for _ in range(contexts - 1)]
    other = [next(it) for _ in range(contexts - 1)]
    wparts = [next(it) for _ in range(shards)]
    mparts = [next(it) for _ in range(shards)]
    bcother = next(it)
    cown = next(it)
    cmine = [next(it) for _ in range(contexts - 1)]
    cother = [next(it) for _ in range(contexts - 1)]
    normed, wfull, small, pre, uall, dtraw, ssd, states, cot = (next(it) for _ in range(9))
    wdt, sref, pref = (next(it) for _ in range(3))
    c, t, s = idx[0], idx[1], idx[2]
    length, width = own.shape
    half = length // 2
    total = length * contexts
    rows = width // shards
    bcw = 2 * state
    for k in range(shards):
        at = pl.multiple_of((s ^ k) * rows, rows)
        part = mparts[k]
        wfull[pl.ds(at, rows), 0:channels] = wparts[k][...]
        here, there = part[:, 0:state], bcother[k]
        wfull[pl.ds(at, rows), channels : channels + state] = jnp.where(t == 0, here, there)
        wfull[pl.ds(at, rows), channels + state : channels + bcw] = jnp.where(t == 0, there, here)
        wfull[pl.ds(at, rows), channels + bcw :] = part[:, state:]
    assemble_tokens(cot, idx, cown, cmine, cother)
    misc = wfull[:, channels + bcw :]
    small[0:MISC, :] = mm(misc, spread_head(width, shards, channels, head), 0, 0)
    small[MISC:, :] = mm(misc, spread_bc(width, shards, bcw), 0, 0)
    expand = (iota((MISC, channels), 0) == high(iota((MISC, channels), 1), head)).astype(f32)
    wdt[...] = mm(misc, expand.astype(bf16)).astype(bf16)
    gain = mm(one_hot(8, MISC, 0, GAIN), misc, 1, 1)[0:1, :]

    def norm(tokens):
        x = tokens.astype(f32)
        return (x * lax.rsqrt(jnp.mean(x * x, -1, keepdims=True) + eps) * gain).astype(bf16)

    for q in range(length // SPAN):
        normed[pl.ds(pl.multiple_of(c * length + q * SPAN, SPAN), SPAN), :] = norm(
            own[q * SPAN : (q + 1) * SPAN, :]
        )
    for k in range(1, contexts):
        base = (c ^ k) * length
        normed[pl.ds(pl.multiple_of(base + t * half, half), half), :] = norm(mine[k - 1][...])
        normed[pl.ds(pl.multiple_of(base + (1 - t) * half, half), half), :] = norm(other[k - 1][...])
    pref[0:PAD, :] = jnp.zeros((PAD, channels + bcw), f32)
    pre[0:PAD, :] = jnp.zeros((PAD, channels + bcw), bf16)
    chunk = 2 * SPAN

    def project(i, _):
        at = pl.multiple_of(i * chunk, chunk)
        n = normed[pl.ds(at, chunk), :]
        value = mm(n, wfull[:, 0 : channels + bcw]).astype(bf16)
        pre[pl.ds(pl.multiple_of(at + PAD, PAD), chunk), :] = value
        pref[pl.ds(pl.multiple_of(at + PAD, PAD), chunk), :] = value.astype(f32)
        dtraw[pl.ds(at, chunk), :] = mm(n, wdt[...])
        return 0

    lax.fori_loop(0, total // chunk, project, 0)
    sref[...] = jnp.zeros_like(sref)
    tri = triangle(True)
    causal = iota((SPAN, SPAN), 0) >= iota((SPAN, SPAN), 1)
    side = iota((SPAN, 2 * head), 1) < head

    def scan(i, _):
        at = pl.multiple_of(i * SPAN, SPAN)
        window = pref[pl.ds(at, SPAN + PAD), :]
        mk = masks[pl.ds(at, SPAN), :]
        taps = jnp.concatenate(
            [small[HEADP : HEADP + 8, :], small[MISC + BCP : MISC + BCP + 8, :]], 1
        )
        u = taps[CONV - 1 : CONV, :] * window[PAD:, :]
        bias = jnp.concatenate(
            [small[HEADP + 4 : HEADP + 5, :], small[MISC + BCP + 4 : MISC + BCP + 5, :]], 1
        )
        u = u + bias
        for j in range(1, CONV):
            u = u + taps[CONV - 1 - j : CONV - j, :] * (
                window[PAD - j : PAD - j + SPAN, :] * mk[:, j - 1 : j]
            )
        uall[pl.ds(at, SPAN), :] = u
        act = u * sigmoid(u)
        x = act[:, 0:channels]
        bfull, cfull = act[:, channels : channels + state], act[:, channels + state :]
        bb, cb = bfull.astype(bf16), cfull.astype(bf16)
        dt = softplus(dtraw[pl.ds(at, SPAN), :] + rates[0:1, :])
        a = exact_left(tri, rates[1:2, :] * dt, 3)
        att = a.T
        step = x * dt
        ub = step.astype(bf16)
        g = mm3(cfull, bfull, 1, 1)
        keep = (mk[:, 5:6] == segr[pl.ds(i, 1), :]) & causal
        inner = []
        for pair in range(channels // (2 * head)):
            up = ub[:, pair * 2 * head : (pair + 1) * 2 * head]
            both = [
                mm((g * local_decay(keep, a, att, head, 2 * pair + e)).astype(bf16), up)
                for e in range(2)
            ]
            inner.append(jnp.where(side, both[0], both[1]))
        before = sref[...]
        sb = before.astype(bf16)
        states[pl.ds(pl.multiple_of(i * channels, channels), channels), :] = sb
        carry = jnp.exp(a) * mk[:, 3:4]
        y = jnp.concatenate(inner, 1) + carry * mm(cb, sb, 1, 1)
        ssd[pl.ds(at, SPAN), :] = y + rates[2:3, :] * x
        tail = jnp.exp(a[SPAN - 1 :, :] - a) * mk[:, 4:5]
        through = jnp.exp(att[:, SPAN - 1 :]) * mk[SPAN - 1 :, 3:4]
        sref[...] = through * before + mm((tail * step).astype(bf16), bb, 0, 0)
        return 0

    lax.fori_loop(0, total // SPAN, scan, 0)


def assemble_tokens(dst, idx, own, mine, other):
    c, t = idx[0], idx[1]
    length = own.shape[0]
    half = length // 2
    dst[pl.ds(pl.multiple_of(c * length, length), length), :] = own[...]
    for k in range(1, len(mine) + 1):
        base = (c ^ k) * length
        dst[pl.ds(pl.multiple_of(base + t * half, half), half), :] = mine[k - 1][...]
        dst[pl.ds(pl.multiple_of(base + (1 - t) * half, half), half), :] = other[k - 1][...]


def gate_kernel(dims, *refs):
    shards, _, _, channels, _ = dims
    it = iter(refs)
    idx = next(it)
    normed, ssd, small, cot = next(it), next(it), next(it), next(it)
    wparts = [next(it) for _ in range(shards)]
    sums, wzo, zval, dyn = (next(it) for _ in range(4))
    s = idx[2]
    width = normed.shape[1]
    rows = width // shards
    for k in range(shards):
        wzo[pl.ds(pl.multiple_of((s ^ k) * rows, rows), rows), :] = wparts[k][...]
    chunk = 2 * SPAN
    ogain = small[HEADP + 5 : HEADP + 6, :]
    ones = jnp.ones((8, channels), bf16)
    for i in range(normed.shape[0] // chunk):
        at = slice(i * chunk, (i + 1) * chunk)
        z = mm(normed[at, :], wzo[:, 0:channels])
        d = mm(cot[at, :], wzo[:, channels:])
        zval[at, :] = z
        dyn[at, :] = d
        gated = ssd[at, :] * (z * sigmoid(z))
        sums[0:1, at] = exact_left(ones, gated * gated, 2, 1)[0:1, :]
        sums[1:2, at] = exact_left(ones, d * ogain * gated, 2, 1)[0:1, :]


def mid_kernel(dims, inner, *refs):
    shards, _, _, channels, _ = dims
    it = iter(refs)
    idx = next(it)
    sums, normed, ssd, small, cot, wzo, zval, dyn = (next(it) for _ in range(8))
    okeep, osend, dz, dssd, ogg, ngz = (next(it) for _ in range(6))
    gparts = [next(it) for _ in range(shards)]
    yref = next(it)
    t, s = idx[1], idx[2]
    total, width = normed.shape
    rows = width // shards
    part = width // 2
    chunk = 2 * SPAN
    ogain = small[HEADP + 5 : HEADP + 6, :]
    first = (iota((8, channels), 0) == 0).astype(f32).astype(bf16)
    second = (iota((8, channels), 0) == 1).astype(f32).astype(bf16)
    gacc = jnp.zeros((1, channels), f32)
    keep_at = pl.multiple_of(t * part, part)
    send_at = pl.multiple_of((1 - t) * part, part)
    for i in range(total // chunk):
        at = slice(i * chunk, (i + 1) * chunk)
        pair = jnp.concatenate([sums[:, at], jnp.zeros((6, chunk), f32)], 0)
        square = exact_right(pair, first, 3, 0, 0)
        cross = exact_right(pair, second, 3, 0, 0)
        z = zval[at, :]
        sg = sigmoid(z)
        zs = z * sg
        out = ssd[at, :]
        gated = out * zs
        r = lax.rsqrt(square / inner + eps)
        ynorm = (gated * r * ogain).astype(bf16)
        yref[at, :] = ynorm
        okeep[at, :] = mm(ynorm, wzo[pl.ds(keep_at, part), channels:], 1, 1).astype(bf16)
        osend[at, :] = mm(ynorm, wzo[pl.ds(send_at, part), channels:], 1, 1).astype(bf16)
        d = dyn[at, :]
        dgated = r * (d * ogain) - gated * (r * r * r) * (cross / inner)
        dssd[at, :] = dgated * zs
        dz[at, :] = (dgated * out * (sg * (1.0 + z * (1.0 - sg)))).astype(bf16)
        gacc = gacc + jnp.sum(d * gated * r, 0, keepdims=True)
    ogg[...] = jnp.broadcast_to(gacc, ogg.shape)
    for k in range(shards):
        at = pl.multiple_of((s ^ k) * rows, MISC)
        gz = mm(normed[:, pl.ds(at, rows)], dz[...], 0, 0)
        wrows = pl.ds(pl.multiple_of((s ^ k) * rows, rows), rows)
        dots = jnp.sum(gz * wzo[wrows, 0:channels].astype(f32), -1, keepdims=True)
        ngz[wrows, :] = jnp.broadcast_to(dots, (rows, MISC))
        gparts[k][:, 0:channels] = gz.astype(bf16)
        gparts[k][:, channels:] = mm(cot[:, pl.ds(at, rows)], yref[...], 0, 0).astype(bf16)


def scan_kernel(dims, *refs):
    _, _, head, channels, state = dims
    it = iter(refs)
    idx = next(it)
    segr, masks, rates = next(it), next(it), next(it)
    small, pre, uall, dtraw, ssd, states, dssd = (next(it) for _ in range(7))
    dcat, acc, dsref = (next(it) for _ in range(3))
    total = uall.shape[0]
    bcw = 2 * state
    cat = channels + bcw
    blocks = total // SPAN
    dsref[...] = jnp.zeros_like(dsref)
    acc[...] = jnp.zeros_like(acc)
    lower, upper = triangle(True), triangle(False)
    ones = block_ones(channels, head)
    causal = iota((SPAN, SPAN), 0) >= iota((SPAN, SPAN), 1)
    side = iota((SPAN, 2 * head), 1) < head
    last = iota((SPAN, channels), 0) == SPAN - 1
    sel = (
        iota((channels, MISC), 0) == iota((channels, MISC), 1) * head
    ).astype(f32).astype(bf16)
    row8 = jnp.ones((8, state), bf16)

    def step(ii, halo):
        i = blocks - 1 - ii
        at = pl.multiple_of(i * SPAN, SPAN)
        here = pl.ds(at, SPAN)
        mk = masks[pl.ds(at, SPAN + PAD), :]
        mh = mk[0:SPAN, :]
        u = uall[here, :]
        sg = sigmoid(u)
        act = u * sg
        x = act[:, 0:channels]
        bfull, cfull = act[:, channels : channels + state], act[:, channels + state :]
        bb, cb = bfull.astype(bf16), cfull.astype(bf16)
        raw = dtraw[here, :] + rates[0:1, :]
        dt = softplus(raw)
        dec = rates[1:2, :] * dt
        a = exact_left(lower, dec, 3)
        att = a.T
        us = x * dt
        ub = us.astype(bf16)
        dy = dssd[here, :]
        dyb = dy.astype(bf16)
        g = mm3(cfull, bfull, 1, 1)
        keep = (mh[:, 5:6] == segr[pl.ds(i, 1), :]) & causal
        carry = jnp.exp(a) * mh[:, 3:4]
        tail = jnp.exp(a[SPAN - 1 :, :] - a) * mh[:, 4:5]
        sb = states[pl.ds(pl.multiple_of(i * channels, channels), channels), :]
        nxt = jnp.minimum(i + 1, blocks - 1)
        snext = states[pl.ds(pl.multiple_of(nxt * channels, channels), channels), :].astype(f32)
        dsn = dsref[...]
        dsb = dsn.astype(bf16)
        cdy = carry * dy
        tu = tail * us
        dg = jnp.zeros((SPAN, SPAN), f32)
        dus = []
        for pair in range(channels // (2 * head)):
            lanes = slice(pair * 2 * head, (pair + 1) * 2 * head)
            dyp = dyb[:, lanes]
            both = []
            for e in range(2):
                decay = local_decay(keep, a, att, head, 2 * pair + e)
                mine = side if e == 0 else jnp.logical_not(side)
                dm = mm3(dy[:, lanes], jnp.where(mine, us[:, lanes], 0.0), 1, 1)
                dg = dg + dm * decay
                both.append(mm((g * decay).astype(bf16), dyp, 0, 0))
            dus.append(jnp.where(side, both[0], both[1]))
        dc = mm3(dg, bfull) + exact_right(cdy, sb, 2)
        db = mm3(dg, cfull, 0, 0) + mm3(tu, dsn)
        du = jnp.concatenate(dus, 1) + tail * mm(bb, dsb, 1, 1)
        through = jnp.exp(att[:, SPAN - 1 :]) * mh[SPAN - 1 :, 3:4]
        dsref[...] = through * dsn + mm(cdy.astype(bf16), cb, 0, 0)
        y = ssd[here, :] - rates[2:3, :] * x
        extra = exact_left(row8, snext * dsn, 3, 1)[0:1, :]
        e = dyb.astype(f32) * y - ub.astype(f32) * du
        e = e + jnp.where(last, extra, 0.0)
        ddec = exact_right(exact_left(upper, e, 3), ones, 3)
        xdu = exact_right(x * du, ones, 2)
        ddt = (xdu + rates[1:2, :] * ddec) * sigmoid(raw)
        acc[8:9, :] = acc[8:9, :] + jnp.sum(ddt, 0, keepdims=True)
        acc[9:10, :] = acc[9:10, :] + jnp.sum(ddec * dec, 0, keepdims=True)
        acc[10:11, :] = acc[10:11, :] + jnp.sum(dy * x, 0, keepdims=True)
        dx = dt * du + rates[2:3, :] * dy
        dact = jnp.concatenate([dx, db, dc], 1)
        dut = dact * (sg * (1.0 + u * (1.0 - sg)))
        dwin = jnp.concatenate([dut, halo], 0)
        pwin = pre[pl.ds(at, SPAN + PAD), :].astype(f32)
        taps = jnp.concatenate(
            [small[HEADP : HEADP + 8, :], small[MISC + BCP : MISC + BCP + 8, :]], 1
        )
        dpre = taps[CONV - 1 : CONV, :] * dut

        def gather(row, value):
            total_row = jnp.sum(value, 0, keepdims=True)
            acc[row : row + 1, :] = acc[row : row + 1, :] + total_row[:, 0:channels]
            acc[16 + row : 17 + row, 0:bcw] = acc[16 + row : 17 + row, 0:bcw] + total_row[:, channels:]

        gather(CONV - 1, dut * pwin[PAD:, :])
        gather(CONV, dut)
        for j in range(1, CONV):
            moved = dwin * mk[:, j - 1 : j]
            dpre = dpre + taps[CONV - 1 - j : CONV - j, :] * moved[j : j + SPAN, :]
            gather(CONV - 1 - j, moved[0:SPAN, :] * pwin[PAD - j : PAD - j + SPAN, :])
        dcat[here, 0:cat] = dpre.astype(bf16)
        dcat[here, cat:] = mm(ddt.astype(bf16), sel).astype(bf16)
        return dut[0:PAD, :]

    lax.fori_loop(0, blocks, step, jnp.zeros((PAD, cat), f32))
    acc[8:16, :] = jnp.where(
        iota((8, channels), 0) == 2, exact_right(acc[8:16, :], ones, 3), acc[8:16, :]
    )


def token_kernel(dims, *refs):
    _, _, _, channels, _ = dims
    idx, wfull, wzo, dz, dcat, dkeep, dsend = refs
    t = idx[1]
    total, width = dcat.shape[0], wfull.shape[0]
    part = width // 2
    chunk = 2 * SPAN
    for i in range(total // chunk):
        at = slice(i * chunk, (i + 1) * chunk)
        full = mm(dcat[at, :], wfull[...], 1, 1) + mm(dz[at, :], wzo[:, 0:channels], 1, 1)
        lo, hi = full[:, 0:part].astype(bf16), full[:, part:].astype(bf16)
        dkeep[at, :] = jnp.where(t == 0, lo, hi)
        dsend[at, :] = jnp.where(t == 0, hi, lo)


def weight_kernel(dims, *refs):
    shards, _, head, channels, state = dims
    idx, normed, wfull, dcat, acc, ogg, ngz, gkeep, gsend = refs
    t = idx[1]
    width = wfull.shape[0]
    bcw = 2 * state
    cat = channels + bcw
    chunk = 2 * SPAN
    headg = jnp.where(iota((8, channels), 0) == 5, ogg[0:8, :], acc[0:8, :])
    z8 = jnp.zeros((8, channels), f32)

    def place(rowsets, spread):
        stack = [z8] * (MISC // 8)
        for row, value in rowsets:
            stack[row // 8] = value
        return mm(spread, jnp.concatenate(stack, 0).astype(bf16), 1, 1)

    misc = place([(HEADP, headg)], spread_head(width, shards, channels, head))
    bch, bcl = pieces(acc[16:24, 0:bcw], 2)
    misc = misc + place(
        [(BCP, bch.astype(f32)), (BCLO, bcl.astype(f32))], spread_bc(width, shards, bcw)
    )
    misc = misc + place([(RATE, acc[8:16, :])], spread_rate(width, shards, channels, head))
    gain_lane = (iota((1, MISC), 1) == GAIN).astype(f32)
    for i in range(width // chunk):
        at = slice(i * chunk, (i + 1) * chunk)
        gw = mm(normed[:, at], dcat[...], 0, 0)
        w = wfull[at, :].astype(f32)
        ng = jnp.sum(gw * w, -1, keepdims=True) + ngz[at, 0:1]
        ng = ng / w[:, cat + GAIN : cat + GAIN + 1]
        gkeep[at, 0:channels] = gw[:, 0:channels].astype(bf16)
        b, c = gw[:, channels : channels + state], gw[:, channels + state : cat]
        gkeep[at, channels : channels + state] = jnp.where(t == 0, b, c).astype(bf16)
        gsend[at, 0:state] = jnp.where(t == 0, c, b).astype(bf16)
        m = (gw[:, cat:] + misc[at, :] + ng * gain_lane).astype(bf16)
        gkeep[at, channels + state :] = m
        gsend[at, state:] = m


def outer_kernel(dims, *refs):
    _, contexts, _, channels, _ = dims
    idx, parts, out = refs[0], refs[1:-1], refs[-1]
    for k in range(contexts):
        at = pl.multiple_of((idx[0] ^ k) * channels, channels)
        out[pl.ds(at, channels), :] = parts[k][:, channels:].astype(f32).T


def final_kernel(dims, *refs):
    shards, contexts, head, channels, state = dims
    idx = refs[0]
    zparts, xparts = refs[1 : 1 + contexts], refs[1 + contexts : 1 + 2 * contexts]
    gi, dt, ng, cw, cb, og, bcc, bcb, ra, rb, rc = refs[1 + 2 * contexts :]
    c = idx[0]
    rows = gi.shape[0]
    heads = channels // head
    piece = head // shards
    span = heads * piece
    every = contexts * span
    names = contexts * heads
    pick = iota((8, MISC), 1)
    line = iota((8, MISC), 0)
    bcsel = ((pick == line + BCP) | (pick == line + BCLO)) & (line < 5)
    bcsel = bcsel.astype(f32).astype(bf16)
    gsel = one_hot(8, MISC, 0, GAIN)
    dts = jnp.zeros((rows, names), f32)
    gains = jnp.zeros((8, rows), f32)
    bcs = jnp.zeros((8, rows), f32)
    small = jnp.zeros((MISC, every), f32)
    rates = jnp.zeros((MISC, names), f32)
    for k in range(contexts):
        place = c ^ k
        at = pl.multiple_of(place * channels, channels)
        gi[:, 0, pl.ds(at, channels)] = zparts[k][:, 0:channels].astype(f32)
        gi[:, 1, pl.ds(at, channels)] = xparts[k][:, 0:channels].astype(f32)
        m = xparts[k][:, channels + state :]

        def to_lane(count, width, size):
            r, q = iota((count, width), 0), iota((count, width), 1)
            return ((q == place * size + r) & (r < size)).astype(f32).astype(bf16)

        dts = dts + mm(m, to_lane(MISC, names, heads))
        gains = gains + mm(gsel, m, 1, 1)
        bcs = bcs + mm(bcsel, m, 1, 1)
        small = small + mm(m, to_lane(rows, every, span), 0, 0)
        rates = rates + mm(m, to_lane(rows, names, heads), 0, 0)
    dt[...] = dts
    ng[...] = gains[0:1, :]
    bcc[...] = bcs[0:CONV, 0 : bcc.shape[1]]
    bcb[...] = bcs[CONV : CONV + 1, 0 : bcb.shape[1]]
    mine = high(iota((names, every), 1), piece) == iota((names, every), 0)
    fold = (low(iota((every, piece), 0), piece) == iota((every, piece), 1)).astype(f32).astype(bf16)

    def split(row):
        return mm(jnp.where(mine, small[row : row + 1, :], 0.0).astype(bf16), fold)

    for j in range(CONV):
        cw[j] = split(HEADP + j)
    cb[...] = split(HEADP + CONV)
    og[...] = split(HEADP + CONV + 1)
    for j, ref in enumerate((ra, rb, rc)):
        ref[...] = rates[RATE + j : RATE + j + 1, :]


def swap(x, axis, k):
    return lax.ppermute(x, axis, [(i, i ^ k) for i in range(lax.axis_size(axis))])


def call(cost, body, args, outs, scratch):
    smem = pl.BlockSpec(memory_space=pltpu.SMEM)
    vmem = pl.BlockSpec(memory_space=pltpu.VMEM)
    return launch(cost, body, args, outs, scratch, smem, vmem)


def launch(cost, body, args, outs, scratch, smem, vmem):
    return pl.pallas_call(
        body,
        cost_estimate=pl.CostEstimate(flops=cost * 10**9, transcendentals=0, bytes_accessed=1 << 20),
        out_shape=[jax.ShapeDtypeStruct(s, d) for s, d in outs],
        in_specs=[smem] + [vmem] * (len(args) - 1),
        out_specs=[vmem] * len(outs),
        scratch_shapes=[pltpu.VMEM(s, d) for s, d in scratch],
        compiler_params=pltpu.CompilerParams(vmem_limit_bytes=56 << 20),
    )(*args)


def stream_parts(rows, core, contexts):
    half = rows.shape[0] // 2
    mine = lax.dynamic_slice_in_dim(rows, core * half, half, 0)
    return [swap(mine, "context", k) for k in range(1, contexts)]


def layer(
    tokens,
    segment_ids,
    norm_gain,
    in_proj,
    bc_proj,
    dt_proj,
    conv_weight,
    conv_bias,
    bc_conv,
    bc_bias,
    dt_bias,
    a_log,
    d_skip,
    out_gain,
    out_proj,
    cotangent,
):
    shards, contexts = lax.axis_size("shard"), lax.axis_size("context")
    s, c, t = lax.axis_index("shard"), lax.axis_index("context"), lax.axis_index("tensor")
    idx = jnp.stack([c, t, s]).astype(jnp.int32)
    length, width = tokens.shape[1:]
    total = length * contexts
    rows = in_proj.shape[0]
    heads = dt_bias.shape[0] // contexts
    state = bc_proj.shape[1] // 2
    bcw = 2 * state
    channels = in_proj.shape[2] // contexts
    head = channels // heads
    inner = in_proj.shape[2] * lax.axis_size("tensor")
    dims = (shards, contexts, head, channels, state)
    own, cot = tokens[0], cotangent[0]

    def mine(x, dim, size):
        return lax.dynamic_slice_in_dim(x, c * size, size, dim)

    tok_mine = stream_parts(own, t, contexts)
    both = lax.dynamic_slice(in_proj, (0, 0, c * channels), (rows, 2, channels))
    hparts = [
        mine(conv_weight, 1, heads).reshape(CONV, -1),
        mine(conv_bias, 0, heads).reshape(1, -1),
        mine(out_gain, 0, heads).reshape(1, -1),
    ]
    headp = jnp.concatenate(hparts, 0).T
    bcp = jnp.concatenate([bc_conv, bc_bias[None]], 0).T

    def column(x, at):
        return jnp.pad(x, ((0, rows - x.shape[0]), (at, MISC - at - x.shape[1])))

    misc = (
        column(mine(dt_proj, 1, heads), 0)
        + column(norm_gain[:, None], GAIN)
        + column(headp, HEADP)
        + column(bcp, BCP)
    )
    wx = both[:, 1]
    wx_parts = [wx] + [swap(wx, "shard", k) for k in range(1, shards)]
    wm = jnp.concatenate([lax.dynamic_slice_in_dim(bc_proj, t * state, state, 1), misc], 1)
    wm_parts = [wm] + [swap(wm, "shard", k) for k in range(1, shards)]
    bc_other = swap(jnp.stack([w[:, :state] for w in wm_parts]), "tensor", 1)
    tok_other = [swap(x, "tensor", 1) for x in tok_mine]
    cot_mine = stream_parts(cot, t, contexts)
    wo = mine(out_proj, 0, channels).T
    wb = jnp.concatenate([both[:, 0], wo], 1)
    wb_parts = [wb] + [swap(wb, "shard", k) for k in range(1, shards)]
    cot_other = [swap(x, "tensor", 1) for x in cot_mine]

    seg = segment_ids[0]
    cols = []
    for j in range(1, CONV):
        moved = jnp.concatenate([jnp.full((j,), -1, jnp.int32), seg[:-j]])
        cols.append((moved == seg).astype(f32))
    grid = seg.reshape(total // SPAN, SPAN)
    previous = jnp.concatenate([jnp.full((1,), -1, jnp.int32), grid[:-1, -1]])
    cols.append((grid == previous[:, None]).astype(f32).reshape(-1))
    cols.append((grid == grid[:, -1:]).astype(f32).reshape(-1))
    cols.append(seg.astype(f32))
    masks = jnp.pad(jnp.stack(cols, 1), ((0, PAD), (0, 2)))
    segr = grid.astype(f32)
    rates = jnp.stack([mine(dt_bias, 0, heads), -jnp.exp(mine(a_log, 0, heads)), mine(d_skip, 0, heads)])
    rates = jnp.pad(jnp.repeat(rates, head, axis=1), ((0, 5), (0, 0)))

    cat = channels + bcw
    front = call(
        15,
        lambda *r: front_kernel(dims, *r),
        [idx, segr, masks, rates, own]
        + tok_mine
        + tok_other
        + wx_parts
        + wm_parts
        + [bc_other, cot]
        + cot_mine
        + cot_other,
        [
            ((total, width), bf16),
            ((width, cat + MISC), bf16),
            ((2 * MISC, channels), f32),
            ((total + PAD, cat), bf16),
            ((total, cat), f32),
            ((total, channels), f32),
            ((total, channels), f32),
            ((total // SPAN * channels, state), bf16),
            ((total, width), bf16),
        ],
        [((width, channels), bf16), ((channels, state), f32), ((total + PAD, cat), f32)],
    )
    normed, wfull, small, pre, uall, dtraw, ssd, states, cotfull = front
    sums, wzo, zval, dyn = call(
        7,
        lambda *r: gate_kernel(dims, *r),
        [idx, normed, ssd, small, cotfull] + wb_parts,
        [
            ((2, total), f32),
            ((width, 2 * channels), bf16),
            ((total, channels), f32),
            ((total, channels), f32),
        ],
        [],
    )
    sums = sums + swap(sums, "tensor", 1)
    k = 1
    while k < contexts:
        sums = sums + swap(sums, "context", k)
        k *= 2
    part = width // 2
    mid = call(
        8,
        lambda *r: mid_kernel(dims, inner, *r),
        [idx, sums, normed, ssd, small, cotfull, wzo, zval, dyn],
        [
            ((total, part), bf16),
            ((total, part), bf16),
            ((total, channels), bf16),
            ((total, channels), f32),
            ((8, channels), f32),
            ((width, MISC), f32),
        ]
        + [((rows, 2 * channels), bf16)] * shards,
        [((total, channels), bf16)],
    )
    okeep, osend, dz, dssd, ogg, ngz = mid[:6]
    zo = mid[6:]

    def stream_reduce(keep, send):
        away = swap(send, "tensor", 1)
        full = keep.astype(f32) + away.astype(f32)

        def rows_of(k):
            return lax.dynamic_slice_in_dim(full, (c ^ k) * length, length, 0)

        got = [swap(rows_of(k).astype(bf16), "context", k) for k in range(1, contexts)]
        return rows_of(0) + sum(g.astype(f32) for g in got)

    def shard_reduce(parts):
        got = [swap(parts[k], "shard", k) for k in range(1, shards)]
        return (parts[0].astype(f32) + sum(g.astype(f32) for g in got)).astype(bf16)

    def context_gather(x):
        return [x] + [swap(x, "context", k) for k in range(1, contexts)]

    mixed = stream_reduce(okeep, osend)
    residual = lax.dynamic_slice_in_dim(own, t * part, part, 1).astype(f32)
    block_out = (residual + mixed).astype(bf16)[None]
    zo_all = context_gather(shard_reduce(zo))

    dcat, acc = call(
        22,
        lambda *r: scan_kernel(dims, *r),
        [idx, segr, masks, rates, small, pre, uall, dtraw, ssd, states, dssd],
        [((total, cat + MISC), bf16), ((24, channels), f32)],
        [((channels, state), f32)],
    )
    gkeep, gsend = call(
        4,
        lambda *r: weight_kernel(dims, *r),
        [idx, normed, wfull, dcat, acc, ogg, ngz],
        [((width, channels + state + MISC), bf16), ((width, state + MISC), bf16)],
        [],
    )
    dkeep, dsend = call(
        4,
        lambda *r: token_kernel(dims, *r),
        [idx, wfull, wzo, dz, dcat],
        [((total, part), bf16), ((total, part), bf16)],
        [],
    )
    lane = jnp.arange(MISC)
    common = (lane == GAIN) | ((lane >= BCP) & (lane < BCLO + 8))
    grecv = swap(gsend, "tensor", 1).astype(f32)
    grecv = jnp.concatenate([grecv[:, :state], jnp.where(common, grecv[:, state:], 0.0)], 1)
    gfull = gkeep.astype(f32) + jnp.pad(grecv, ((0, 0), (channels, 0)))
    gparts = [
        lax.dynamic_slice_in_dim(gfull, (s ^ k) * rows, rows, 0).astype(bf16) for k in range(shards)
    ]
    fx = context_gather(shard_reduce(gparts))
    dpart = stream_reduce(dkeep, dsend)
    dpart = dpart.astype(bf16)
    dother = swap(dpart, "tensor", 1)
    dnormed = jnp.concatenate(
        [jnp.where(t == 0, dpart, dother), jnp.where(t == 0, dother, dpart)], 1
    ).astype(f32)

    xfloat = own.astype(f32)
    gain_full = wfull[:, cat + GAIN].astype(f32)
    rstd = lax.rsqrt(jnp.mean(xfloat * xfloat, -1, keepdims=True) + eps)
    weighted = dnormed * gain_full
    dx = rstd * weighted - xfloat * rstd**3 * jnp.mean(weighted * xfloat, -1, keepdims=True)
    tokens_grad = (cot.astype(f32) + dx)[None]

    (outproj_grad,) = call(
        2,
        lambda *r: outer_kernel(dims, *r),
        [idx] + zo_all,
        [((contexts * channels, rows), f32)],
        [],
    )
    shared = sum(p[:, channels : channels + state].astype(f32) for p in fx)
    bc_half = shared.astype(bf16)
    bc_away = swap(bc_half, "tensor", 1)
    bcproj_grad = jnp.concatenate(
        [jnp.where(t == 0, bc_half, bc_away), jnp.where(t == 0, bc_away, bc_half)], 1
    ).astype(f32)
    piece = head // shards
    names = contexts * heads
    final = call(
        4,
        lambda *r: final_kernel(dims, *r),
        [idx] + zo_all + fx,
        [
            ((rows, 2, contexts * channels), f32),
            ((rows, names), f32),
            ((1, rows), f32),
            ((CONV, names, piece), f32),
            ((names, piece), f32),
            ((names, piece), f32),
            ((CONV, bcw // shards), f32),
            ((1, bcw // shards), f32),
            ((1, names), f32),
            ((1, names), f32),
            ((1, names), f32),
        ],
        [],
    )
    inproj_grad, dtproj_grad, ng, convw_grad, convb_grad, outgain_grad, bcconv_grad = final[:7]
    return (
        block_out,
        tokens_grad,
        ng.reshape(-1),
        inproj_grad,
        bcproj_grad,
        dtproj_grad,
        convw_grad,
        convb_grad,
        bcconv_grad,
        final[7].reshape(-1),
        final[8].reshape(-1),
        final[9].reshape(-1),
        final[10].reshape(-1),
        outgain_grad,
        outproj_grad,
    )


def solution(mesh):
    return jax.shard_map(
        layer,
        mesh=mesh,
        in_specs=(
            P("shard", "context", None),
            P("shard", None),
            P("shard"),
            P("shard", None, "tensor"),
            P("shard", None),
            P("shard", "tensor"),
            P(None, "tensor", "shard"),
            P("tensor", "shard"),
            P(None, "shard"),
            P("shard"),
            P("tensor"),
            P("tensor"),
            P("tensor"),
            P("tensor", "shard"),
            P("tensor", "shard"),
            P("shard", "context", None),
        ),
        out_specs=(
            P("shard", "context", "tensor"),
            P("shard", "context", None),
            P("shard"),
            P("shard", None, "tensor"),
            P("shard", None),
            P("shard", "tensor"),
            P(None, "tensor", "shard"),
            P("tensor", "shard"),
            P(None, "shard"),
            P("shard"),
            P("tensor"),
            P("tensor"),
            P("tensor"),
            P("tensor", "shard"),
            P("tensor", "shard"),
        ),
        check_vma=False,
    )
```

profile of v0, /device:TPU:0, one launch (start us, length us, event | category | flops | bytes accessed | tf_op | source)
XLA Modules:
  0.0 231.2 jit_solution(11480940291566335110)
XLA Ops:
  6.1 5.1 %collective-permute-start.11 = (bf16[256,256]{1,0:T(8,128)(2,1)S(1)}, bf16[256,256]{1,0:T(8,128)(2,1)S(1)}, u32[]{:S(2)}, u32[]{:S(2)}) collective-permute-start(bf16[256,256]{1,0:T(8,128)(2,1)S(1)} %pad_maximum_fusion.2.r_15_), channel_id=1, source_target_pairs={{0,24},{8,16},{16,8},{24,0},{1,25},{9,17},{17,9},{25,1},{2,26},{10... | collective-permute-start | bytes 393224 | tf_op jit(solution)/shard_map/ppermute | solution.py:553
  15.0 2.9 %collective-permute-start.7 = (bf16[256,256]{1,0:T(8,128)(2,1)S(1)}, bf16[256,256]{1,0:T(8,128)(2,1)S(1)}, u32[]{:S(2)}, u32[]{:S(2)}) collective-permute-start(bf16[256,256]{1,0:T(8,128)(2,1)S(1)} %bitcast.77), channel_id=1, source_target_pairs={{0,16},{8,24},{16,0},{24,8},{1,17},{9,25},{17,1},{25,9},{2,18},{10... | collective-permute-start | bytes 393224 | tf_op jit(solution)/shard_map/ppermute | solution.py:553
  19.4 4.7 %collective-permute-done.10.r_17_ = bf16[256,256]{1,0:T(8,128)(2,1)S(1)} collective-permute-done((bf16[256,256]{1,0:T(8,128)(2,1)S(1)}, bf16[256,256]{1,0:T(8,128)(2,1)S(1)}, u32[]{:S(2)}, u32[]{:S(2)}) %collective-permute-start.10) | collective-permute-done | bytes 131104 | tf_op jit(solution)/shard_map/ppermute | solution.py:553
  28.1 3.6 %collective-permute-done.7.r_13_ = bf16[256,256]{1,0:T(8,128)(2,1)S(1)} collective-permute-done((bf16[256,256]{1,0:T(8,128)(2,1)S(1)}, bf16[256,256]{1,0:T(8,128)(2,1)S(1)}, u32[]{:S(2)}, u32[]{:S(2)}) %collective-permute-start.7) | collective-permute-done | bytes 131104 | tf_op jit(solution)/shard_map/ppermute | solution.py:553
  35.2 3.9 %collective-permute-done.15.r_23_ = bf16[128,1024]{1,0:T(8,128)(2,1)S(1)} collective-permute-done((bf16[128,1024]{1,0:T(8,128)(2,1)S(1)}, bf16[128,1024]{1,0:T(8,128)(2,1)S(1)}, u32[]{:S(2)}, u32[]{:S(2)}) %collective-permute-start.15) | collective-permute-done | bytes 262176 | tf_op jit(solution)/shard_map/ppermute | solution.py:553
  39.4 4.3 %collective-permute-done.r_5_ = bf16[128,1024]{1,0:T(8,128)(2,1)S(1)} collective-permute-done((bf16[128,1024]{1,0:T(8,128)(2,1)S(1)}, bf16[128,1024]{1,0:T(8,128)(2,1)S(1)}, u32[]{:S(2)}, u32[]{:S(2)}) %collective-permute-start) | collective-permute-done | bytes 262176 | tf_op jit(solution)/shard_map/ppermute | solution.py:553
  43.7 4.3 %collective-permute-done.1.r_6_ = bf16[128,1024]{1,0:T(8,128)(2,1)} collective-permute-done((bf16[128,1024]{1,0:T(8,128)(2,1)S(1)}, bf16[128,1024]{1,0:T(8,128)(2,1)}, u32[]{:S(2)}, u32[]{:S(2)}) %collective-permute-start.1) | collective-permute-done | bytes 262176 | tf_op jit(solution)/shard_map/ppermute | solution.py:553
  53.4 3.0 %collective-permute-start.20 = (bf16[256,512]{1,0:T(8,128)(2,1)S(1)}, bf16[256,512]{1,0:T(8,128)(2,1)S(1)}, u32[]{:S(2)}, u32[]{:S(2)}) collective-permute-start(bf16[256,512]{1,0:T(8,128)(2,1)S(1)} %pad_maximum_fusion.1.r_5_), channel_id=1, source_target_pairs={{0,16},{8,24},{16,0},{24,8},{1,17},{9,25},{17,1},{25,9},{2,18},{10... | collective-permute-start | bytes 786440 | tf_op jit(solution)/shard_map/ppermute | solution.py:553
  57.1 16.8 %shard_map.271 = (bf16[1024,1024]{1,0:T(8,128)(2,1)}, bf16[1024,640]{1,0:T(8,128)(2,1)}, f32[256,256]{1,0:T(8,128)}, bf16[1040,512]{1,0:T(8,128)(2,1)}, f32[1024...) custom-call(s32[3]{0:T(128)} %pad_add_fusion.1.r_0_, ...), custom_call_target="tpu_custom_call" | custom-call | flops 15000000512 | bytes 1048576 | tf_op jit(solution)/shard_map/pallas_call | solution.py:563
  75.6 6.5 %shard_map.272 = (f32[2,1024]{1,0:T(2,128)}, bf16[1024,512]{1,0:T(8,128)(2,1)}, f32[1024,256]{1,0:T(8,128)}, f32[1024,256]{1,0:T(8,128)}) custom-call(s32[3]{0:T(128)} %pad_add_fusion.1.r_0_, bf16[1024,1024]{1,0:T(8,128)(2,1)} %get-tuple-element.55.r_1_.r_2_, f32[1024,256]{1,0:T(8,128)} %get-tuple-element.56.r_2_.r_3_.r_8_, ...), custom_call_target="tpu_custom_call" | custom-call | flops 7000000000 | bytes 1048576 | tf_op jit(solution)/shard_map/pallas_call | solution.py:563
  92.2 8.6 %shard_map.273 = (bf16[1024,512]{1,0:T(8,128)(2,1)}, bf16[1024,512]{1,0:T(8,128)(2,1)}, bf16[1024,256]{1,0:T(8,128)(2,1)}, f32[1024,256]{1,0:T(8,128)}, f32[8,25...) custom-call(s32[3]{0:T(128)} %pad_add_fusion.1.r_0_, ...), custom_call_target="tpu_custom_call" | custom-call | flops 8000000000 | bytes 1048576 | tf_op jit(solution)/shard_map/pallas_call | solution.py:563
  100.7 21.8 %shard_map.274 = (bf16[1024,640]{1,0:T(8,128)(2,1)}, f32[24,256]{1,0:T(8,128)}) custom-call(s32[3]{0:T(128)} %pad_add_fusion.1.r_0_, f32[8,128]{1,0:T(8,128)} %convert_element_type.219.r_1_, f32[1040,8]{1,0:T(8,128)} %pad.30.r_2_, f32[8,256]{1,0:T(8,128)} %pad.31.r_3_, f32[256,256]{1,0:T(8,128)} %get-tuple-element.57.r_3_.r_4_, ...), custom_call_target="tpu_custom_call" | custom-call | flops 22000001024 | bytes 1048576 | tf_op jit(solution)/shard_map/pallas_call | solution.py:563
  122.6 6.1 %shard_map.276 = (bf16[1024,512]{1,0:T(8,128)(2,1)}, bf16[1024,256]{1,0:T(8,128)(2,1)}) custom-call(s32[3]{0:T(128)} %pad_add_fusion.1.r_0_, bf16[1024,1024]{1,0:T(8,128)(2,1)} %get-tuple-element.55.r_1_.r_2_, bf16[1024,640]{1,0:T(8,128)(2,1)} %get-tuple-element.65.r_1_.r_2_, bf16[1024,640]{1,0:T(8,128)(2,1)} %get-tuple-element.72.r_4_.r_3_, ...), custom_call_target="tpu_custom_call" | custom-call | flops 4000000000 | bytes 1048576 | tf_op jit(solution)/shard_map/pallas_call | solution.py:563
  128.7 5.7 %collective-permute-start.34 = (bf16[256,512]{1,0:T(8,128)(2,1)}, bf16[256,512]{1,0:T(8,128)(2,1)S(1)}, u32[]{:S(2)}, u32[]{:S(2)}) collective-permute-start(bf16[256,512]{1,0:T(8,128)(2,1)} %get-tuple-element.76), channel_id=1, source_target_pairs={{0,8},{8,0},{16,24},{24,16},{1,9},{9,1},{17,25},{25,17},{2,10},{10... | collective-permute-start | bytes 786440 | tf_op jit(solution)/shard_map/ppermute | solution.py:553
  139.0 5.9 %shard_map.275 = (bf16[1024,512]{1,0:T(8,128)(2,1)}, bf16[1024,512]{1,0:T(8,128)(2,1)}) custom-call(s32[3]{0:T(128)} %pad_add_fusion.1.r_0_, bf16[1024,640]{1,0:T(8,128)(2,1)} %get-tuple-element.65.r_1_.r_2_, bf16[1024,512]{1,0:T(8,128)(2,1)} %get-tuple-element.60.r_6_.r_2_, bf16[1024,256]{1,0:T(8,128)(2,1)} %get-tuple-element.66.r_3_, ...), custom_call_target="tpu_custom_call" | custom-call | flops 4000000000 | bytes 1048576 | tf_op jit(solution)/shard_map/pallas_call | solution.py:563
  147.0 8.8 %collective-permute-done.35 = bf16[256,512]{1,0:T(8,128)(2,1)S(1)} collective-permute-done((bf16[256,512]{1,0:T(8,128)(2,1)S(1)}, bf16[256,512]{1,0:T(8,128)(2,1)S(1)}, u32[]{:S(2)}, u32[]{:S(2)}) %collective-permute-start.35) | collective-permute-done | bytes 262176 | tf_op jit(solution)/shard_map/ppermute | solution.py:553
  155.8 2.4 %collective-permute-start.43 = (bf16[256,512]{1,0:T(8,128)(2,1)S(1)}, bf16[256,512]{1,0:T(8,128)(2,1)}, u32[]{:S(2)}, u32[]{:S(2)}) collective-permute-start(bf16[256,512]{1,0:T(8,128)(2,1)S(1)} %get-tuple-element.149), channel_id=1, source_target_pairs={{0,24},{8,16},{16,8},{24,0},{1,25},{9,17},{17,9},{25,1},{2,26},{10... | collective-permute-start | bytes 786440 | tf_op jit(solution)/shard_map/ppermute | solution.py:553
  160.5 17.9 %collective-permute-done.42 = bf16[256,512]{1,0:T(8,128)(2,1)} collective-permute-done((bf16[256,512]{1,0:T(8,128)(2,1)}, bf16[256,512]{1,0:T(8,128)(2,1)}, u32[]{:S(2)}, u32[]{:S(2)}) %collective-permute-start.42) | collective-permute-done | bytes 262176 | tf_op jit(solution)/shard_map/ppermute | solution.py:553
  185.9 2.5 %collective-permute-done.39.r_4_ = bf16[256,512]{1,0:T(8,128)(2,1)S(1)} collective-permute-done((bf16[256,512]{1,0:T(8,128)(2,1)S(1)}, bf16[256,512]{1,0:T(8,128)(2,1)S(1)}, u32[]{:S(2)}, u32[]{:S(2)}) %collective-permute-start.39) | collective-permute-done | bytes 262176 | tf_op jit(solution)/shard_map/ppermute | solution.py:553
  191.5 2.6 %collective-permute-done.44.r_6_ = bf16[256,512]{1,0:T(8,128)(2,1)S(1)} collective-permute-done((bf16[256,512]{1,0:T(8,128)(2,1)S(1)}, bf16[256,512]{1,0:T(8,128)(2,1)S(1)}, u32[]{:S(2)}, u32[]{:S(2)}) %collective-permute-start.44) | collective-permute-done | bytes 262176 | tf_op jit(solution)/shard_map/ppermute | solution.py:553
  194.2 3.0 %collective-permute-done.46.r_8_ = bf16[256,512]{1,0:T(8,128)(2,1)S(1)} collective-permute-done((bf16[256,512]{1,0:T(8,128)(2,1)S(1)}, bf16[256,512]{1,0:T(8,128)(2,1)S(1)}, u32[]{:S(2)}, u32[]{:S(2)}) %collective-permute-start.46) | collective-permute-done | bytes 262176 | tf_op jit(solution)/shard_map/ppermute | solution.py:553
  204.3 3.9 %shard_map.277 = (f32[256,2,1024]{2,1,0:T(2,128)}, f32[256,16]{1,0:T(8,128)}, f32[1,256]{1,0:T(1,128)}, f32[4,16,16]{2,1,0:T(8,128)}, f32[16,16]{1,0:T(8,128)}, ...) custom-call(s32[3]{0:T(128)} %pad_add_fusion.1.r_0_, ...), custom_call_target="tpu_custom_call" | custom-call | flops 4000000000 | bytes 1048576 | tf_op jit(solution)/shard_map/pallas_call | solution.py:563
  218.9 2.8 %collective-permute-done.26 = bf16[256,512]{1,0:T(8,128)(2,1)S(1)} collective-permute-done((bf16[256,512]{1,0:T(8,128)(2,1)}, bf16[256,512]{1,0:T(8,128)(2,1)S(1)}, u32[]{:S(2)}, u32[]{:S(2)}) %collective-permute-start.26) | collective-permute-done | bytes 262176 | tf_op jit(solution)/shard_map/ppermute | solution.py:553
  222.7 4.8 %collective-permute-done.28 = bf16[256,512]{1,0:T(8,128)(2,1)S(1)} collective-permute-done((bf16[256,512]{1,0:T(8,128)(2,1)}, bf16[256,512]{1,0:T(8,128)(2,1)S(1)}, u32[]{:S(2)}, u32[]{:S(2)}) %collective-permute-start.28) | collective-permute-done | bytes 262176 | tf_op jit(solution)/shard_map/ppermute | solution.py:553
  (241 shorter events, 77.9 us)
Async XLA Ops:
  11.2 14.6 %collective-permute-start.9 = (bf16[256,256]{1,0:T(8,128)(2,1)S(1)}, bf16[256,256]{1,0:T(8,128)(2,1)S(1)}, u32[]{:S(2)}, u32[]{:S(2)}) collective-permute-start(bf16[256,256]{1,0:T(8,128)(2,1)S(1)} %pad_maximum_fusion.2.r_15_), channel_id=1, source_target_pairs={{0,8},{8,0},{16,24},{24,16},{1,9},{9,1},{17,25},{25,17},{2,10},{10... | collective-permute-start | bytes 393224 | tf_op jit(solution)/shard_map/ppermute | solution.py:553
  13.5 13.9 %collective-permute-start.6 = (bf16[256,256]{1,0:T(8,128)(2,1)S(1)}, bf16[256,256]{1,0:T(8,128)(2,1)S(1)}, u32[]{:S(2)}, u32[]{:S(2)}) collective-permute-start(bf16[256,256]{1,0:T(8,128)(2,1)S(1)} %bitcast.76), channel_id=1, source_target_pairs={{0,8},{8,0},{16,24},{24,16},{1,9},{9,1},{17,25},{25,17},{2,10},{10... | collective-permute-start | bytes 393224 | tf_op jit(solution)/shard_map/ppermute | solution.py:553
  15.0 16.7 %collective-permute-start.7 = (bf16[256,256]{1,0:T(8,128)(2,1)S(1)}, bf16[256,256]{1,0:T(8,128)(2,1)S(1)}, u32[]{:S(2)}, u32[]{:S(2)}) collective-permute-start(bf16[256,256]{1,0:T(8,128)(2,1)S(1)} %bitcast.77), channel_id=1, source_target_pairs={{0,16},{8,24},{16,0},{24,8},{1,17},{9,25},{17,1},{25,9},{2,18},{10... | collective-permute-start | bytes 393224 | tf_op jit(solution)/shard_map/ppermute | solution.py:553
  18.7 14.5 %collective-permute-start.8 = (bf16[256,256]{1,0:T(8,128)(2,1)S(1)}, bf16[256,256]{1,0:T(8,128)(2,1)S(1)}, u32[]{:S(2)}, u32[]{:S(2)}) collective-permute-start(bf16[256,256]{1,0:T(8,128)(2,1)S(1)} %bitcast.78), channel_id=1, source_target_pairs={{0,24},{8,16},{16,8},{24,0},{1,25},{9,17},{17,9},{25,1},{2,26},{10... | collective-permute-start | bytes 393224 | tf_op jit(solution)/shard_map/ppermute | solution.py:553
  33.2 14.7 %collective-permute-start.1 = (bf16[128,1024]{1,0:T(8,128)(2,1)S(1)}, bf16[128,1024]{1,0:T(8,128)(2,1)}, u32[]{:S(2)}, u32[]{:S(2)}) collective-permute-start(bf16[128,1024]{1,0:T(8,128)(2,1)S(1)} %dynamic-slice_bitcast_fusion.1), channel_id=1, source_target_pairs={{0,4},{2,6},{4,0},{6,2},{1,5},{3,7},{5,1},{7,3},{8,12},{10,14},{12... | collective-permute-start | bytes 786440 | tf_op jit(solution)/shard_map/ppermute | solution.py:553
  35.2 13.2 %collective-permute-start.12 = (bf16[4,256,128]{2,1,0:T(8,128)(2,1)S(1)}, bf16[4,256,128]{2,1,0:T(8,128)(2,1)S(1)}, u32[]{:S(2)}, u32[]{:S(2)}) collective-permute-start(bf16[4,256,128]{2,1,0:T(8,128)(2,1)S(1)} %pad_maximum_fusion), channel_id=1, source_target_pairs={{0,1},{1,0},{2,3},{3,2},{4,5},{5,4},{6,7},{7,6},{8,9},{9,8},{10,11... | collective-permute-start | bytes 786440 | tf_op jit(solution)/shard_map/ppermute | solution.py:553
  52.6 21.3 %collective-permute-start.19 = (bf16[256,512]{1,0:T(8,128)(2,1)S(1)}, bf16[256,512]{1,0:T(8,128)(2,1)S(1)}, u32[]{:S(2)}, u32[]{:S(2)}) collective-permute-start(bf16[256,512]{1,0:T(8,128)(2,1)S(1)} %pad_maximum_fusion.1.r_5_), channel_id=1, source_target_pairs={{0,8},{8,0},{16,24},{24,16},{1,9},{9,1},{17,25},{25,17},{2,10},{10... | collective-permute-start | bytes 786440 | tf_op jit(solution)/shard_map/ppermute | solution.py:553
  53.4 21.5 %collective-permute-start.20 = (bf16[256,512]{1,0:T(8,128)(2,1)S(1)}, bf16[256,512]{1,0:T(8,128)(2,1)S(1)}, u32[]{:S(2)}, u32[]{:S(2)}) collective-permute-start(bf16[256,512]{1,0:T(8,128)(2,1)S(1)} %pad_maximum_fusion.1.r_5_), channel_id=1, source_target_pairs={{0,16},{8,24},{16,0},{24,8},{1,17},{9,25},{17,1},{25,9},{2,18},{10... | collective-permute-start | bytes 786440 | tf_op jit(solution)/shard_map/ppermute | solution.py:553
  56.4 18.4 %collective-permute-start.21 = (bf16[256,512]{1,0:T(8,128)(2,1)S(1)}, bf16[256,512]{1,0:T(8,128)(2,1)S(1)}, u32[]{:S(2)}, u32[]{:S(2)}) collective-permute-start(bf16[256,512]{1,0:T(8,128)(2,1)S(1)} %pad_maximum_fusion.1.r_5_), channel_id=1, source_target_pairs={{0,24},{8,16},{16,8},{24,0},{1,25},{9,17},{17,9},{25,1},{2,26},{10... | collective-permute-start | bytes 786440 | tf_op jit(solution)/shard_map/ppermute | solution.py:553
  128.7 18.2 %collective-permute-start.34 = (bf16[256,512]{1,0:T(8,128)(2,1)}, bf16[256,512]{1,0:T(8,128)(2,1)S(1)}, u32[]{:S(2)}, u32[]{:S(2)}) collective-permute-start(bf16[256,512]{1,0:T(8,128)(2,1)} %get-tuple-element.76), channel_id=1, source_target_pairs={{0,8},{8,0},{16,24},{24,16},{1,9},{9,1},{17,25},{25,17},{2,10},{10... | collective-permute-start | bytes 786440 | tf_op jit(solution)/shard_map/ppermute | solution.py:553
  134.4 21.4 %collective-permute-start.35 = (bf16[256,512]{1,0:T(8,128)(2,1)S(1)}, bf16[256,512]{1,0:T(8,128)(2,1)S(1)}, u32[]{:S(2)}, u32[]{:S(2)}) collective-permute-start(bf16[256,512]{1,0:T(8,128)(2,1)S(1)} %copy-done.34), channel_id=1, source_target_pairs={{0,16},{8,24},{16,0},{24,8},{1,17},{9,25},{17,1},{25,9},{2,18},{10... | collective-permute-start | bytes 786440 | tf_op jit(solution)/shard_map/ppermute | solution.py:553
  135.4 22.8 %collective-permute-start.36 = (bf16[256,512]{1,0:T(8,128)(2,1)S(1)}, bf16[256,512]{1,0:T(8,128)(2,1)S(1)}, u32[]{:S(2)}, u32[]{:S(2)}) collective-permute-start(bf16[256,512]{1,0:T(8,128)(2,1)S(1)} %copy-done.33), channel_id=1, source_target_pairs={{0,24},{8,16},{16,8},{24,0},{1,25},{9,17},{17,9},{25,1},{2,26},{10... | collective-permute-start | bytes 786440 | tf_op jit(solution)/shard_map/ppermute | solution.py:553
  138.0 20.9 %collective-permute-start.41 = (bf16[256,512]{1,0:T(8,128)(2,1)S(1)}, bf16[256,512]{1,0:T(8,128)(2,1)}, u32[]{:S(2)}, u32[]{:S(2)}) collective-permute-start(bf16[256,512]{1,0:T(8,128)(2,1)S(1)} %get-tuple-element.148), channel_id=1, source_target_pairs={{0,8},{8,0},{16,24},{24,16},{1,9},{9,1},{17,25},{25,17},{2,10},{10... | collective-permute-start | bytes 786440 | tf_op jit(solution)/shard_map/ppermute | solution.py:553
  145.0 52.4 %collective-permute-start.29 = (bf16[1024,512]{1,0:T(8,128)(2,1)}, bf16[1024,512]{1,0:T(8,128)(2,1)S(1)}, u32[]{:S(2)}, u32[]{:S(2)}) collective-permute-start(bf16[1024,512]{1,0:T(8,128)(2,1)} %get-tuple-element.74), channel_id=1, source_target_pairs={{0,1},{1,0},{2,3},{3,2},{4,5},{5,4},{6,7},{7,6},{8,9},{9,8},{10,11... | collective-permute-start | bytes 3145736 | tf_op jit(solution)/shard_map/ppermute | solution.py:553
  147.0 31.4 %collective-permute-start.42 = (bf16[256,512]{1,0:T(8,128)(2,1)}, bf16[256,512]{1,0:T(8,128)(2,1)}, u32[]{:S(2)}, u32[]{:S(2)}) collective-permute-start(bf16[256,512]{1,0:T(8,128)(2,1)} %get-tuple-element.150), channel_id=1, source_target_pairs={{0,16},{8,24},{16,0},{24,8},{1,17},{9,25},{17,1},{25,9},{2,18},{10... | collective-permute-start | bytes 786440 | tf_op jit(solution)/shard_map/ppermute | solution.py:553
  155.8 24.1 %collective-permute-start.43 = (bf16[256,512]{1,0:T(8,128)(2,1)S(1)}, bf16[256,512]{1,0:T(8,128)(2,1)}, u32[]{:S(2)}, u32[]{:S(2)}) collective-permute-start(bf16[256,512]{1,0:T(8,128)(2,1)S(1)} %get-tuple-element.149), channel_id=1, source_target_pairs={{0,24},{8,16},{16,8},{24,0},{1,25},{9,17},{17,9},{25,1},{2,26},{10... | collective-permute-start | bytes 786440 | tf_op jit(solution)/shard_map/ppermute | solution.py:553
  158.4 24.4 %collective-permute-start.37 = (bf16[256,512]{1,0:T(8,128)(2,1)S(1)}, bf16[256,512]{1,0:T(8,128)(2,1)S(1)}, u32[]{:S(2)}, u32[]{:S(2)}) collective-permute-start(bf16[256,512]{1,0:T(8,128)(2,1)S(1)} %add_convert_fusion.1.r_1_), channel_id=1, source_target_pairs={{0,2},{2,0},{4,6},{6,4},{1,3},{3,1},{5,7},{7,5},{8,10},{10,8},{12,... | collective-permute-start | bytes 786440 | tf_op jit(solution)/shard_map/ppermute | solution.py:553
  158.9 24.3 %collective-permute-start.38 = (bf16[256,512]{1,0:T(8,128)(2,1)S(1)}, bf16[256,512]{1,0:T(8,128)(2,1)}, u32[]{:S(2)}, u32[]{:S(2)}) collective-permute-start(bf16[256,512]{1,0:T(8,128)(2,1)S(1)} %add_convert_fusion.1.r_1_), channel_id=1, source_target_pairs={{0,4},{2,6},{4,0},{6,2},{1,5},{3,7},{5,1},{7,3},{8,12},{10,14},{12... | collective-permute-start | bytes 786440 | tf_op jit(solution)/shard_map/ppermute | solution.py:553
  183.2 13.9 %collective-permute-start.46 = (bf16[256,512]{1,0:T(8,128)(2,1)S(1)}, bf16[256,512]{1,0:T(8,128)(2,1)S(1)}, u32[]{:S(2)}, u32[]{:S(2)}) collective-permute-start(bf16[256,512]{1,0:T(8,128)(2,1)S(1)} %add_convert_fusion.r_5_), channel_id=1, source_target_pairs={{0,6},{2,4},{4,2},{6,0},{1,7},{3,5},{5,3},{7,1},{8,14},{10,12},{12... | collective-permute-start | bytes 786440 | tf_op jit(solution)/shard_map/ppermute | solution.py:553
  188.5 19.7 %collective-permute-start.25 = (bf16[1024,512]{1,0:T(8,128)(2,1)}, bf16[1024,512]{1,0:T(8,128)(2,1)S(1)}, u32[]{:S(2)}, u32[]{:S(2)}) collective-permute-start(bf16[1024,512]{1,0:T(8,128)(2,1)} %get-tuple-element.64), channel_id=1, source_target_pairs={{0,1},{1,0},{2,3},{3,2},{4,5},{5,4},{6,7},{7,6},{8,9},{9,8},{10,11... | collective-permute-start | bytes 3145736 | tf_op jit(solution)/shard_map/ppermute | solution.py:553
  197.2 16.2 %collective-permute-start.47 = (bf16[256,128]{1,0:T(8,128)(2,1)S(1)}, bf16[256,128]{1,0:T(8,128)(2,1)S(1)}, u32[]{:S(2)}, u32[]{:S(2)}) collective-permute-start(bf16[256,128]{1,0:T(8,128)(2,1)S(1)} %add_convert_fusion.3), channel_id=1, source_target_pairs={{0,1},{1,0},{2,3},{3,2},{4,5},{5,4},{6,7},{7,6},{8,9},{9,8},{10,11... | collective-permute-start | bytes 196616 | tf_op jit(solution)/shard_map/ppermute | solution.py:553
  200.8 13.6 %collective-permute-start.30 = (bf16[256,512]{1,0:T(8,128)(2,1)}, bf16[256,512]{1,0:T(8,128)(2,1)}, u32[]{:S(2)}, u32[]{:S(2)}) collective-permute-start(bf16[256,512]{1,0:T(8,128)(2,1)} %get-tuple-element.142), channel_id=1, source_target_pairs={{0,2},{2,0},{4,6},{6,4},{1,3},{3,1},{5,7},{7,5},{8,10},{10,8},{12,... | collective-permute-start | bytes 786440 | tf_op jit(solution)/shard_map/ppermute | solution.py:553
  201.9 14.0 %collective-permute-start.31 = (bf16[256,512]{1,0:T(8,128)(2,1)}, bf16[256,512]{1,0:T(8,128)(2,1)}, u32[]{:S(2)}, u32[]{:S(2)}) collective-permute-start(bf16[256,512]{1,0:T(8,128)(2,1)} %get-tuple-element.144), channel_id=1, source_target_pairs={{0,4},{2,6},{4,0},{6,2},{1,5},{3,7},{5,1},{7,3},{8,12},{10,14},{12... | collective-permute-start | bytes 786440 | tf_op jit(solution)/shard_map/ppermute | solution.py:553
  202.8 14.0 %collective-permute-start.32 = (bf16[256,512]{1,0:T(8,128)(2,1)S(1)}, bf16[256,512]{1,0:T(8,128)(2,1)}, u32[]{:S(2)}, u32[]{:S(2)}) collective-permute-start(bf16[256,512]{1,0:T(8,128)(2,1)S(1)} %get-tuple-element.143), channel_id=1, source_target_pairs={{0,6},{2,4},{4,2},{6,0},{1,7},{3,5},{5,3},{7,1},{8,14},{10,12},{12... | collective-permute-start | bytes 786440 | tf_op jit(solution)/shard_map/ppermute | solution.py:553
  (67 other events, 866.7 us)
where the time goes:
time: 232 us; the launch traced here: 231 us
  waiting for transfers between devices  73.9 us (32%)
  Pallas kernels  72 us (31%)
  starting transfers between devices  52.3 us (23%)
  local copies, waits for them, and re-layouts  17.5 us (8%)
  other arithmetic  14.2 us (6%)
    ppermute x48, waiting for transfers between devices, swap(): lax.ppermute(x, axis, [(i, i ^ k) for i in range(lax.axis_size(axis))])  73.9 us
    pallas_call x8, Pallas kernels, launch(): pl.pallas_call(body, cost_estimate=pl.CostEstimate(flops=cost * 10 ** 9,...  72 us
    ppermute x48, starting transfers between devices, swap(): lax.ppermute(x, axis, [(i, i ^ k) for i in range(lax.axis_size(axis))])  52.3 us
    unnamed x91, local copies, waits for them, and re-layouts  6.37 us
  transfers between devices with their start and end apart: 48, of which 19 were waited for; matrix products, arithmetic and copies ran while one was open for 8% of the time, Pallas kernels for 13%

commit v1 on v0

--- a/solution.py
+++ b/solution.py
@@ -111,28 +111,62 @@
     return jnp.exp(jnp.where(keep, diff, -1e30))
 
 
+def at_rows(start, size, by):
+    return pl.ds(pl.multiple_of(start, by), size)
+
+
+class Rows:
+    def __init__(self, source, target, sems, size):
+        self.source, self.target, self.sems, self.size = source, target, sems, size
+
+    def copy(self, i):
+        at = at_rows(i * self.size, self.size, self.size)
+        return pltpu.make_async_copy(self.source.at[at], self.target.at[at], self.sems.at[i])
+
+    def start(self, i):
+        self.copy(i).start()
+
+    def wait(self, i):
+        self.copy(i).wait()
+
+
 def front_kernel(dims, *refs):
     shards, contexts, head, channels, state = dims
     it = iter(refs)
     idx = next(it)
     segr, masks, rates = next(it), next(it), next(it)
     own = next(it)
+    cown = next(it)
     mine = [next(it) for _ in range(contexts - 1)]
     other = [next(it) for _ in range(contexts - 1)]
     wparts = [next(it) for _ in range(shards)]
     mparts = [next(it) for _ in range(shards)]
     bcother = next(it)
-    cown = next(it)
-    cmine = [next(it) for _ in range(contexts - 1)]
-    cother = [next(it) for _ in range(contexts - 1)]
-    normed, wfull, small, pre, uall, dtraw, ssd, states, cot = (next(it) for _ in range(9))
-    wdt, sref, pref = (next(it) for _ in range(3))
+    small, *houts, cot = (next(it) for _ in range(9))
+    wdt, sref, pref, xtok, xcot = (next(it) for _ in range(5))
+    normed, wfull, pre, uall, dtraw, ssd, states = (next(it) for _ in range(7))
+    tsem, csem, nsem, psem, vsem, once = (next(it) for _ in range(6))
+    put_cot = pltpu.make_async_copy(xcot, cot, once.at[2])
+    hnormed, hwfull, hpre, huall, hdtraw, hssd, hstates = houts
     c, t, s = idx[0], idx[1], idx[2]
     length, width = own.shape
     half = length // 2
     total = length * contexts
     rows = width // shards
     bcw = 2 * state
+    spans = [(at_rows(c * length, length, length), own, cown)]
+    for k in range(1, contexts):
+        base = (c ^ k) * length
+        spans.append((at_rows(base + t * half, half, half), mine[k - 1], None))
+        spans.append((at_rows(base + (1 - t) * half, half, half), other[k - 1], None))
+    loads, moves = [], []
+    for n, (where, token, cots) in enumerate(spans):
+        head_rows = token if cots is not None else token.at[pl.ds(0, half)]
+        tail_rows = cots if cots is not None else token.at[pl.ds(half, half)]
+        loads.append(pltpu.make_async_copy(head_rows, xtok.at[where], tsem.at[n]))
+        moves.append(pltpu.make_async_copy(tail_rows, xcot.at[where], csem.at[n]))
+    for copy in loads + moves:
+        copy.start()
     for k in range(shards):
         at = pl.multiple_of((s ^ k) * rows, rows)
         part = mparts[k]
@@ -141,7 +175,6 @@
         wfull[pl.ds(at, rows), channels : channels + state] = jnp.where(t == 0, here, there)
         wfull[pl.ds(at, rows), channels + state : channels + bcw] = jnp.where(t == 0, there, here)
         wfull[pl.ds(at, rows), channels + bcw :] = part[:, state:]
-    assemble_tokens(cot, idx, cown, cmine, cother)
     misc = wfull[:, channels + bcw :]
     small[0:MISC, :] = mm(misc, spread_head(width, shards, channels, head), 0, 0)
     small[MISC:, :] = mm(misc, spread_bc(width, shards, bcw), 0, 0)
@@ -153,17 +186,32 @@
         x = tokens.astype(f32)
         return (x * lax.rsqrt(jnp.mean(x * x, -1, keepdims=True) + eps) * gain).astype(bf16)
 
-    for q in range(length // SPAN):
-        normed[pl.ds(pl.multiple_of(c * length + q * SPAN, SPAN), SPAN), :] = norm(
-            own[q * SPAN : (q + 1) * SPAN, :]
-        )
-    for k in range(1, contexts):
-        base = (c ^ k) * length
-        normed[pl.ds(pl.multiple_of(base + t * half, half), half), :] = norm(mine[k - 1][...])
-        normed[pl.ds(pl.multiple_of(base + (1 - t) * half, half), half), :] = norm(other[k - 1][...])
+    keep_w = pltpu.make_async_copy(wfull, hwfull, once.at[0])
+    keep_w.start()
+    stores = []
+    for n, (where, _, _) in enumerate(spans):
+        loads[n].wait()
+        normed[where, :] = norm(xtok[where, :])
+        stores.append(pltpu.make_async_copy(normed.at[where], hnormed.at[where], nsem.at[n]))
+        stores[-1].start()
     pref[0:PAD, :] = jnp.zeros((PAD, channels + bcw), f32)
     pre[0:PAD, :] = jnp.zeros((PAD, channels + bcw), bf16)
     chunk = 2 * SPAN
+    chunks = total // chunk
+    blocks = total // SPAN
+    first_pre = pltpu.make_async_copy(
+        pre.at[pl.ds(0, PAD)], hpre.at[pl.ds(0, PAD)], once.at[1]
+    )
+    first_pre.start()
+    rest = pl.ds(PAD, total)
+    for copy in moves:
+        copy.wait()
+    put_cot.start()
+    put_pre = Rows(pre.at[rest], hpre.at[rest], psem.at[0], chunk)
+    put_dt = Rows(dtraw, hdtraw, psem.at[1], chunk)
+    put_u = Rows(uall, huall, vsem.at[0], SPAN)
+    put_ssd = Rows(ssd, hssd, vsem.at[1], SPAN)
+    put_states = Rows(states, hstates, vsem.at[2], channels)
 
     def project(i, _):
         at = pl.multiple_of(i * chunk, chunk)
@@ -172,9 +220,11 @@
         pre[pl.ds(pl.multiple_of(at + PAD, PAD), chunk), :] = value
         pref[pl.ds(pl.multiple_of(at + PAD, PAD), chunk), :] = value.astype(f32)
         dtraw[pl.ds(at, chunk), :] = mm(n, wdt[...])
+        put_pre.start(i)
+        put_dt.start(i)
         return 0
 
-    lax.fori_loop(0, total // chunk, project, 0)
+    lax.fori_loop(0, chunks, project, 0)
     sref[...] = jnp.zeros_like(sref)
     tri = triangle(True)
     causal = iota((SPAN, SPAN), 0) >= iota((SPAN, SPAN), 1)
@@ -225,20 +275,28 @@
         tail = jnp.exp(a[SPAN - 1 :, :] - a) * mk[:, 4:5]
         through = jnp.exp(att[:, SPAN - 1 :]) * mk[SPAN - 1 :, 3:4]
         sref[...] = through * before + mm((tail * step).astype(bf16), bb, 0, 0)
+        put_u.start(i)
+        put_ssd.start(i)
+        put_states.start(i)
         return 0
 
-    lax.fori_loop(0, total // SPAN, scan, 0)
-
-
-def assemble_tokens(dst, idx, own, mine, other):
-    c, t = idx[0], idx[1]
-    length = own.shape[0]
-    half = length // 2
-    dst[pl.ds(pl.multiple_of(c * length, length), length), :] = own[...]
-    for k in range(1, len(mine) + 1):
-        base = (c ^ k) * length
-        dst[pl.ds(pl.multiple_of(base + t * half, half), half), :] = mine[k - 1][...]
-        dst[pl.ds(pl.multiple_of(base + (1 - t) * half, half), half), :] = other[k - 1][...]
+    lax.fori_loop(0, blocks, scan, 0)
+    for copy in stores + [keep_w, first_pre, put_cot]:
+        copy.wait()
+
+    def finish_chunk(i, _):
+        put_pre.wait(i)
+        put_dt.wait(i)
+        return 0
+
+    def finish_block(i, _):
+        put_u.wait(i)
+        put_ssd.wait(i)
+        put_states.wait(i)
+        return 0
+
+    lax.fori_loop(0, chunks, finish_chunk, 0)
+    lax.fori_loop(0, blocks, finish_block, 0)
 
 
 def gate_kernel(dims, *refs):
@@ -274,7 +332,7 @@
     sums, normed, ssd, small, cot, wzo, zval, dyn = (next(it) for _ in range(8))
     okeep, osend, dz, dssd, ogg, ngz = (next(it) for _ in range(6))
     gparts = [next(it) for _ in range(shards)]
-    yref = next(it)
+    yref, gref = next(it), next(it)
     t, s = idx[1], idx[2]
     total, width = normed.shape
     rows = width // shards
@@ -307,14 +365,15 @@
         dz[at, :] = (dgated * out * (sg * (1.0 + z * (1.0 - sg)))).astype(bf16)
         gacc = gacc + jnp.sum(d * gated * r, 0, keepdims=True)
     ogg[...] = jnp.broadcast_to(gacc, ogg.shape)
+    for i in range(width // chunk):
+        at = slice(i * chunk, (i + 1) * chunk)
+        gz = mm(normed[:, at], dz[...], 0, 0)
+        dots = jnp.sum(gz * wzo[at, 0:channels].astype(f32), -1, keepdims=True)
+        ngz[at, :] = jnp.broadcast_to(dots, (chunk, MISC))
+        gref[at, 0:channels] = gz.astype(bf16)
+        gref[at, channels:] = mm(cot[:, at], yref[...], 0, 0).astype(bf16)
     for k in range(shards):
-        at = pl.multiple_of((s ^ k) * rows, MISC)
-        gz = mm(normed[:, pl.ds(at, rows)], dz[...], 0, 0)
-        wrows = pl.ds(pl.multiple_of((s ^ k) * rows, rows), rows)
-        dots = jnp.sum(gz * wzo[wrows, 0:channels].astype(f32), -1, keepdims=True)
-        ngz[wrows, :] = jnp.broadcast_to(dots, (rows, MISC))
-        gparts[k][:, 0:channels] = gz.astype(bf16)
-        gparts[k][:, channels:] = mm(cot[:, pl.ds(at, rows)], yref[...], 0, 0).astype(bf16)
+        gparts[k][...] = gref[pl.ds(pl.multiple_of((s ^ k) * rows, rows), rows), :]
 
 
 def scan_kernel(dims, *refs):
@@ -322,9 +381,21 @@
     it = iter(refs)
     idx = next(it)
     segr, masks, rates = next(it), next(it), next(it)
-    small, pre, uall, dtraw, ssd, states, dssd = (next(it) for _ in range(7))
-    dcat, acc, dsref = (next(it) for _ in range(3))
-    total = uall.shape[0]
+    small, pre, huall, hdtraw, hssd, states, hdssd = (next(it) for _ in range(7))
+    hdcat, acc, dsref = (next(it) for _ in range(3))
+    uall, dtraw, ssd, dssd, dcat, sems, osem = (next(it) for _ in range(7))
+    total = huall.shape[0]
+    count = total // SPAN
+    takes = [
+        Rows(src, dst, sems.at[n], SPAN)
+        for n, (src, dst) in enumerate(
+            ((huall, uall), (hdtraw, dtraw), (hdssd, dssd), (hssd, ssd))
+        )
+    ]
+    give = Rows(dcat, hdcat, osem, SPAN)
+    for i in reversed(range(count)):
+        for take in takes:
+            take.start(i)
     bcw = 2 * state
     cat = channels + bcw
     blocks = total // SPAN
@@ -344,6 +415,8 @@
         i = blocks - 1 - ii
         at = pl.multiple_of(i * SPAN, SPAN)
         here = pl.ds(at, SPAN)
+        for take in takes:
+            take.wait(i)
         mk = masks[pl.ds(at, SPAN + PAD), :]
         mh = mk[0:SPAN, :]
         u = uall[here, :]
@@ -423,12 +496,19 @@
             gather(CONV - 1 - j, moved[0:SPAN, :] * pwin[PAD - j : PAD - j + SPAN, :])
         dcat[here, 0:cat] = dpre.astype(bf16)
         dcat[here, cat:] = mm(ddt.astype(bf16), sel).astype(bf16)
+        give.start(i)
         return dut[0:PAD, :]
 
     lax.fori_loop(0, blocks, step, jnp.zeros((PAD, cat), f32))
     acc[8:16, :] = jnp.where(
         iota((8, channels), 0) == 2, exact_right(acc[8:16, :], ones, 3), acc[8:16, :]
     )
+
+    def finish(i, _):
+        give.wait(i)
+        return 0
+
+    lax.fori_loop(0, blocks, finish, 0)
 
 
 def token_kernel(dims, *refs):
@@ -448,9 +528,11 @@
 
 def weight_kernel(dims, *refs):
     shards, _, head, channels, state = dims
-    idx, normed, wfull, dcat, acc, ogg, ngz, gkeep, gsend = refs
-    t = idx[1]
+    idx, normed, wfull, dcat, acc, ogg, ngz, gkeep, gsend = refs[:9]
+    gparts, gref = refs[9:-1], refs[-1]
+    t, s = idx[1], idx[2]
     width = wfull.shape[0]
+    rows = width // shards
     bcw = 2 * state
     cat = channels + bcw
     chunk = 2 * SPAN
@@ -476,13 +558,15 @@
         w = wfull[at, :].astype(f32)
         ng = jnp.sum(gw * w, -1, keepdims=True) + ngz[at, 0:1]
         ng = ng / w[:, cat + GAIN : cat + GAIN + 1]
-        gkeep[at, 0:channels] = gw[:, 0:channels].astype(bf16)
+        gref[at, :] = gw[:, 0:channels].astype(bf16)
         b, c = gw[:, channels : channels + state], gw[:, channels + state : cat]
-        gkeep[at, channels : channels + state] = jnp.where(t == 0, b, c).astype(bf16)
+        gkeep[at, 0:state] = jnp.where(t == 0, b, c).astype(bf16)
         gsend[at, 0:state] = jnp.where(t == 0, c, b).astype(bf16)
         m = (gw[:, cat:] + misc[at, :] + ng * gain_lane).astype(bf16)
-        gkeep[at, channels + state :] = m
+        gkeep[at, state:] = m
         gsend[at, state:] = m
+    for k in range(shards):
+        gparts[k][...] = gref[pl.ds(pl.multiple_of((s ^ k) * rows, rows), rows), :]
 
 
 def outer_kernel(dims, *refs):
@@ -510,7 +594,7 @@
     bcsel = ((pick == line + BCP) | (pick == line + BCLO)) & (line < 5)
     bcsel = bcsel.astype(f32).astype(bf16)
     gsel = one_hot(8, MISC, 0, GAIN)
-    dts = jnp.zeros((rows, names), f32)
+    dts = jnp.zeros((names, rows), f32)
     gains = jnp.zeros((8, rows), f32)
     bcs = jnp.zeros((8, rows), f32)
     small = jnp.zeros((MISC, every), f32)
@@ -526,7 +610,9 @@
             r, q = iota((count, width), 0), iota((count, width), 1)
             return ((q == place * size + r) & (r < size)).astype(f32).astype(bf16)
 
-        dts = dts + mm(m, to_lane(MISC, names, heads))
+        r, q = iota((names, MISC), 0), iota((names, MISC), 1)
+        lift = ((r == place * heads + q) & (q < heads)).astype(f32).astype(bf16)
+        dts = dts + mm(lift, m, 1, 1)
         gains = gains + mm(gsel, m, 1, 1)
         bcs = bcs + mm(bcsel, m, 1, 1)
         small = small + mm(m, to_lane(rows, every, span), 0, 0)
@@ -553,28 +639,27 @@
     return lax.ppermute(x, axis, [(i, i ^ k) for i in range(lax.axis_size(axis))])
 
 
-def call(cost, body, args, outs, scratch):
+def call(cost, body, args, outs, scratch, far_in=(), far_out=()):
     smem = pl.BlockSpec(memory_space=pltpu.SMEM)
     vmem = pl.BlockSpec(memory_space=pltpu.VMEM)
-    return launch(cost, body, args, outs, scratch, smem, vmem)
-
-
-def launch(cost, body, args, outs, scratch, smem, vmem):
+    far = pl.BlockSpec(memory_space=pl.ANY)
+    ins = [smem] + [far if i in far_in else vmem for i in range(1, len(args))]
+    out = [far if i in far_out else vmem for i in range(len(outs))]
+    return launch(cost, body, args, outs, scratch, ins, out)
+
+
+def launch(cost, body, args, outs, scratch, ins, out):
     return pl.pallas_call(
         body,
         cost_estimate=pl.CostEstimate(flops=cost * 10**9, transcendentals=0, bytes_accessed=1 << 20),
         out_shape=[jax.ShapeDtypeStruct(s, d) for s, d in outs],
-        in_specs=[smem] + [vmem] * (len(args) - 1),
-        out_specs=[vmem] * len(outs),
-        scratch_shapes=[pltpu.VMEM(s, d) for s, d in scratch],
+        in_specs=ins,
+        out_specs=out,
+        scratch_shapes=[
+            pltpu.SemaphoreType.DMA(s) if d is None else pltpu.VMEM(s, d) for s, d in scratch
+        ],
         compiler_params=pltpu.CompilerParams(vmem_limit_bytes=56 << 20),
     )(*args)
-
-
-def stream_parts(rows, core, contexts):
-    half = rows.shape[0] // 2
-    mine = lax.dynamic_slice_in_dim(rows, core * half, half, 0)
-    return [swap(mine, "context", k) for k in range(1, contexts)]
 
 
 def layer(
@@ -613,7 +698,11 @@
     def mine(x, dim, size):
         return lax.dynamic_slice_in_dim(x, c * size, size, dim)
 
-    tok_mine = stream_parts(own, t, contexts)
+    half = length // 2
+    pair = jnp.concatenate(
+        [lax.dynamic_slice_in_dim(x, t * half, half, 0) for x in (own, cot)], 0
+    )
+    tok_mine = [swap(pair, "context", k) for k in range(1, contexts)]
     both = lax.dynamic_slice(in_proj, (0, 0, c * channels), (rows, 2, channels))
     hparts = [
         mine(conv_weight, 1, heads).reshape(CONV, -1),
@@ -638,11 +727,9 @@
     wm_parts = [wm] + [swap(wm, "shard", k) for k in range(1, shards)]
     bc_other = swap(jnp.stack([w[:, :state] for w in wm_parts]), "tensor", 1)
     tok_other = [swap(x, "tensor", 1) for x in tok_mine]
-    cot_mine = stream_parts(cot, t, contexts)
     wo = mine(out_proj, 0, channels).T
     wb = jnp.concatenate([both[:, 0], wo], 1)
     wb_parts = [wb] + [swap(wb, "shard", k) for k in range(1, shards)]
-    cot_other = [swap(x, "tensor", 1) for x in cot_mine]
 
     seg = segment_ids[0]
     cols = []
@@ -660,31 +747,45 @@
     rates = jnp.pad(jnp.repeat(rates, head, axis=1), ((0, 5), (0, 0)))
 
     cat = channels + bcw
+    kept = [
+        ((total, width), bf16),
+        ((width, cat + MISC), bf16),
+        ((total + PAD, cat), bf16),
+        ((total, cat), f32),
+        ((total, channels), f32),
+        ((total, channels), f32),
+        ((total // SPAN * channels, state), bf16),
+    ]
     front = call(
         15,
         lambda *r: front_kernel(dims, *r),
-        [idx, segr, masks, rates, own]
+        [idx, segr, masks, rates, own, cot]
         + tok_mine
         + tok_other
         + wx_parts
         + wm_parts
-        + [bc_other, cot]
-        + cot_mine
-        + cot_other,
+        + [bc_other],
+        [((2 * MISC, channels), f32)] + kept + [((total, width), bf16)],
         [
+            ((width, channels), bf16),
+            ((channels, state), f32),
+            ((total + PAD, cat), f32),
             ((total, width), bf16),
-            ((width, cat + MISC), bf16),
-            ((2 * MISC, channels), f32),
-            ((total + PAD, cat), bf16),
-            ((total, cat), f32),
-            ((total, channels), f32),
-            ((total, channels), f32),
-            ((total // SPAN * channels, state), bf16),
             ((total, width), bf16),
+        ]
+        + kept
+        + [
+            ((2 * contexts - 1,), None),
+            ((2 * contexts - 1,), None),
+            ((2 * contexts - 1,), None),
+            ((2, total // (2 * SPAN)), None),
+            ((3, total // SPAN), None),
+            ((3,), None),
         ],
-        [((width, channels), bf16), ((channels, state), f32), ((total + PAD, cat), f32)],
-    )
-    normed, wfull, small, pre, uall, dtraw, ssd, states, cotfull = front
+        far_in=range(4, 4 + 2 * contexts),
+        far_out=range(1, 9),
+    )
+    small, normed, wfull, pre, uall, dtraw, ssd, states, cotfull = front
     sums, wzo, zval, dyn = call(
         7,
         lambda *r: gate_kernel(dims, *r),
@@ -716,7 +817,7 @@
             ((width, MISC), f32),
         ]
         + [((rows, 2 * channels), bf16)] * shards,
-        [((total, channels), bf16)],
+        [((total, channels), bf16), ((width, 2 * channels), bf16)],
     )
     okeep, osend, dz, dssd, ogg, ngz = mid[:6]
     zo = mid[6:]
@@ -748,14 +849,25 @@
         lambda *r: scan_kernel(dims, *r),
         [idx, segr, masks, rates, small, pre, uall, dtraw, ssd, states, dssd],
         [((total, cat + MISC), bf16), ((24, channels), f32)],
-        [((channels, state), f32)],
-    )
-    gkeep, gsend = call(
+        [
+            ((channels, state), f32),
+            ((total, cat), f32),
+            ((total, channels), f32),
+            ((total, channels), f32),
+            ((total, channels), f32),
+            ((total, cat + MISC), bf16),
+            ((4, total // SPAN), None),
+            ((total // SPAN,), None),
+        ],
+        far_in=(6, 7, 8, 10),
+        far_out=(0,),
+    )
+    gkeep, gsend, *gx = call(
         4,
         lambda *r: weight_kernel(dims, *r),
         [idx, normed, wfull, dcat, acc, ogg, ngz],
-        [((width, channels + state + MISC), bf16), ((width, state + MISC), bf16)],
-        [],
+        [((width, state + MISC), bf16)] * 2 + [((rows, channels), bf16)] * shards,
+        [((width, channels), bf16)],
     )
     dkeep, dsend = call(
         4,
@@ -768,11 +880,13 @@
     common = (lane == GAIN) | ((lane >= BCP) & (lane < BCLO + 8))
     grecv = swap(gsend, "tensor", 1).astype(f32)
     grecv = jnp.concatenate([grecv[:, :state], jnp.where(common, grecv[:, state:], 0.0)], 1)
-    gfull = gkeep.astype(f32) + jnp.pad(grecv, ((0, 0), (channels, 0)))
+    gfull = gkeep.astype(f32) + grecv
     gparts = [
         lax.dynamic_slice_in_dim(gfull, (s ^ k) * rows, rows, 0).astype(bf16) for k in range(shards)
     ]
-    fx = context_gather(shard_reduce(gparts))
+    gx = shard_reduce(gx)
+    gm = shard_reduce(gparts)
+    fx = context_gather(jnp.concatenate([gx, gm], 1))
     dpart = stream_reduce(dkeep, dsend)
     dpart = dpart.astype(bf16)
     dother = swap(dpart, "tensor", 1)
@@ -808,7 +922,7 @@
         [idx] + zo_all + fx,
         [
             ((rows, 2, contexts * channels), f32),
-            ((rows, names), f32),
+            ((names, rows), f32),
             ((1, rows), f32),
             ((CONV, names, piece), f32),
             ((names, piece), f32),
@@ -828,7 +942,7 @@
         ng.reshape(-1),
         inproj_grad,
         bcproj_grad,
-        dtproj_grad,
+        dtproj_grad.T,
         convw_grad,
         convb_grad,
         bcconv_grad,

time: 232 us -> 229 us (0.987)
  waiting for transfers between devices: 73.9 us -> 81.1 us
  local copies, waits for them, and re-layouts: 17.5 us -> 12 us
  other arithmetic: 14.2 us -> 9.7 us
  Pallas kernels: 72 us -> 69.6 us
    ppermute x48 -> x45, waiting for transfers between devices: 73.9 us -> 81.1 us  [swap(): lax.ppermute(x, axis, [(i, i ^ k) for i in range(lax.axis_size(axis))])]
    unnamed x91 -> x80, local copies, waits for them, and re-layouts: 6.37 us -> 3.21 us
    pallas_call x8, Pallas kernels: 72 us -> 69.6 us  [launch(): pl.pallas_call(body, cost_estimate=pl.CostEstimate(flops=cost * 10 ** 9,...]
    ppermute x48 -> x45, starting transfers between devices: 52.3 us -> 54.3 us  [swap(): lax.ppermute(x, axis, [(i, i ^ k) for i in range(lax.axis_size(axis))])]
  transfers between devices with their start and end apart: 48 -> 45, of which waited for: 19 -> 19; matrix products, arithmetic and copies ran while one was open for 8% -> 5% of each run, Pallas kernels for 13% -> 24%
where the time goes in v1:
time: 229 us; the launch traced here: 228 us
  waiting for transfers between devices  81.1 us (35%)
  Pallas kernels  69.6 us (30%)
  starting transfers between devices  54.3 us (24%)
  local copies, waits for them, and re-layouts  12 us (5%)
  other arithmetic  9.7 us (4%)
    ppermute x45, waiting for transfers between devices, swap(): lax.ppermute(x, axis, [(i, i ^ k) for i in range(lax.axis_size(axis))])  81.1 us
    pallas_call x8, Pallas kernels, launch(): pl.pallas_call(body, cost_estimate=pl.CostEstimate(flops=cost * 10 ** 9,...  69.6 us
    ppermute x45, starting transfers between devices, swap(): lax.ppermute(x, axis, [(i, i ^ k) for i in range(lax.axis_size(axis))])  54.3 us
  transfers between devices with their start and end apart: 45, of which 19 were waited for; matrix products, arithmetic and copies ran while one was open for 5% of the time, Pallas kernels for 24%

profile of v1, /device:TPU:0, one launch (start us, length us, event | category | flops | bytes accessed | tf_op | source)
XLA Modules:
  0.0 228.1 jit_solution(16751105491588557368)
XLA Ops:
  6.1 5.1 %collective-permute-start.11 = (bf16[256,256]{1,0:T(8,128)(2,1)S(1)}, bf16[256,256]{1,0:T(8,128)(2,1)S(1)}, u32[]{:S(2)}, u32[]{:S(2)}) collective-permute-start(bf16[256,256]{1,0:T(8,128)(2,1)S(1)} %pad_maximum_fusion.4.r_16_), channel_id=1, source_target_pairs={{0,24},{8,16},{16,8},{24,0},{1,25},{9,17},{17,9},{25,1},{2,26},{10... | collective-permute-start | bytes 393224 | tf_op jit(solution)/shard_map/ppermute | solution.py:639
  17.6 3.4 %collective-permute-start.9 = (bf16[256,256]{1,0:T(8,128)(2,1)S(1)}, bf16[256,256]{1,0:T(8,128)(2,1)S(1)}, u32[]{:S(2)}, u32[]{:S(2)}) collective-permute-start(bf16[256,256]{1,0:T(8,128)(2,1)S(1)} %pad_maximum_fusion.4.r_16_), channel_id=1, source_target_pairs={{0,8},{8,0},{16,24},{24,16},{1,9},{9,1},{17,25},{25,17},{2,10},{10... | collective-permute-start | bytes 393224 | tf_op jit(solution)/shard_map/ppermute | solution.py:639
  22.4 2.9 %collective-permute-done.9.r_17_ = bf16[256,256]{1,0:T(8,128)(2,1)S(1)} collective-permute-done((bf16[256,256]{1,0:T(8,128)(2,1)S(1)}, bf16[256,256]{1,0:T(8,128)(2,1)S(1)}, u32[]{:S(2)}, u32[]{:S(2)}) %collective-permute-start.9) | collective-permute-done | bytes 131104 | tf_op jit(solution)/shard_map/ppermute | solution.py:639
  28.2 10.1 %collective-permute-done.1.r_7_ = bf16[256,1024]{1,0:T(8,128)(2,1)} collective-permute-done((bf16[256,1024]{1,0:T(8,128)(2,1)S(1)}, bf16[256,1024]{1,0:T(8,128)(2,1)}, u32[]{:S(2)}, u32[]{:S(2)}) %collective-permute-start.1) | collective-permute-done | bytes 524320 | tf_op jit(solution)/shard_map/ppermute | solution.py:639
  44.0 3.0 %collective-permute-done.8.r_15_ = bf16[256,256]{1,0:T(8,128)(2,1)} collective-permute-done((bf16[256,256]{1,0:T(8,128)(2,1)S(1)}, bf16[256,256]{1,0:T(8,128)(2,1)}, u32[]{:S(2)}, u32[]{:S(2)}) %collective-permute-start.8) | collective-permute-done | bytes 131104 | tf_op jit(solution)/shard_map/ppermute | solution.py:639
  52.1 15.1 %shard_map.271 = (f32[256,256]{1,0:T(8,128)}, bf16[1024,1024]{1,0:T(8,128)(2,1)}, bf16[1024,640]{1,0:T(8,128)(2,1)}, bf16[1040,512]{1,0:T(8,128)(2,1)}, f32[1024...) custom-call(s32[3]{0:T(128)} %pad_add_fusion.1.r_0_, ...), custom_call_target="tpu_custom_call" | custom-call | flops 15000000512 | bytes 1048576 | tf_op jit(solution)/shard_map/pallas_call | solution.py:652
  67.2 3.5 %collective-permute-done.14.r_7_ = bf16[256,512]{1,0:T(8,128)(2,1)S(1)} collective-permute-done((bf16[256,512]{1,0:T(8,128)(2,1)S(1)}, bf16[256,512]{1,0:T(8,128)(2,1)S(1)}, u32[]{:S(2)}, u32[]{:S(2)}) %collective-permute-start.14) | collective-permute-done | bytes 262176 | tf_op jit(solution)/shard_map/ppermute | solution.py:639
  71.5 6.5 %shard_map.272 = (f32[2,1024]{1,0:T(2,128)}, bf16[1024,512]{1,0:T(8,128)(2,1)}, f32[1024,256]{1,0:T(8,128)}, f32[1024,256]{1,0:T(8,128)}) custom-call(s32[3]{0:T(128)} %pad_add_fusion.1.r_0_, bf16[1024,1024]{1,0:T(8,128)(2,1)} %get-tuple-element.59.r_1_.r_2_, f32[1024,256]{1,0:T(8,128)} %get-tuple-element.60.r_2_.r_3_.r_8_, ...), custom_call_target="tpu_custom_call" | custom-call | flops 7000000000 | bytes 1048576 | tf_op jit(solution)/shard_map/pallas_call | solution.py:652
  80.8 2.9 %collective-permute-done.17 = f32[2,1024]{1,0:T(2,128)S(1)} collective-permute-done((f32[2,1024]{1,0:T(2,128)S(1)}, f32[2,1024]{1,0:T(2,128)S(1)}, u32[]{:S(2)}, u32[]{:S(2)}) %collective-permute-start.17) | collective-permute-done | bytes 8224 | tf_op jit(solution)/shard_map/ppermute | solution.py:639
  88.0 8.4 %shard_map.273 = (bf16[1024,512]{1,0:T(8,128)(2,1)}, bf16[1024,512]{1,0:T(8,128)(2,1)}, bf16[1024,256]{1,0:T(8,128)(2,1)}, f32[1024,256]{1,0:T(8,128)}, f32[8,25...) custom-call(s32[3]{0:T(128)} %pad_add_fusion.1.r_0_, ...), custom_call_target="tpu_custom_call" | custom-call | flops 8000000000 | bytes 1048576 | tf_op jit(solution)/shard_map/pallas_call | solution.py:652
  96.4 4.8 %collective-permute-start.28 = (bf16[256,512]{1,0:T(8,128)(2,1)}, bf16[256,512]{1,0:T(8,128)(2,1)S(1)}, u32[]{:S(2)}, u32[]{:S(2)}) collective-permute-start(bf16[256,512]{1,0:T(8,128)(2,1)} %get-tuple-element.80), channel_id=1, source_target_pairs={{0,8},{8,0},{16,24},{24,16},{1,9},{9,1},{17,25},{25,17},{2,10},{10... | collective-permute-start | bytes 786440 | tf_op jit(solution)/shard_map/ppermute | solution.py:639
  101.2 21.4 %shard_map.274 = (bf16[1024,640]{1,0:T(8,128)(2,1)}, f32[24,256]{1,0:T(8,128)}) custom-call(s32[3]{0:T(128)} %pad_add_fusion.1.r_0_, f32[8,128]{1,0:T(8,128)} %convert_element_type.232.r_1_, f32[1040,8]{1,0:T(8,128)} %pad.26.r_2_, f32[8,256]{1,0:T(8,128)} %pad.27.r_3_, f32[256,256]{1,0:T(8,128)} %get-tuple-element.61.r_3_.r_4_, ...), custom_call_target="tpu_custom_call" | custom-call | flops 22000001024 | bytes 1048576 | tf_op jit(solution)/shard_map/pallas_call | solution.py:652
  122.6 5.9 %shard_map.276 = (bf16[1024,256]{1,0:T(8,128)(2,1)}, bf16[1024,256]{1,0:T(8,128)(2,1)}, bf16[256,256]{1,0:T(8,128)(2,1)}, bf16[256,256]{1,0:T(8,128)(2,1)}, bf16...) custom-call(s32[3]{0:T(128)} %pad_add_fusion.1.r_0_, bf16[1024,1024]{1,0:T(8,128)(2,1)} %get-tuple-element.59.r_1_.r_2_, ...), custom_call_target="tpu_custom_call" | custom-call | flops 4000000000 | bytes 1048576 | tf_op jit(solution)/shard_map/pallas_call | solution.py:652
  128.6 3.2 %collective-permute-start.35 = (bf16[256,256]{1,0:T(8,128)(2,1)}, bf16[256,256]{1,0:T(8,128)(2,1)S(1)}, u32[]{:S(2)}, u32[]{:S(2)}) collective-permute-start(bf16[256,256]{1,0:T(8,128)(2,1)} %get-tuple-element.88), channel_id=1, source_target_pairs={{0,16},{8,24},{16,0},{24,8},{1,17},{9,25},{17,1},{25,9},{2,18},{10... | collective-permute-start | bytes 393224 | tf_op jit(solution)/shard_map/ppermute | solution.py:639
  133.0 6.0 %shard_map.275 = (bf16[1024,512]{1,0:T(8,128)(2,1)}, bf16[1024,512]{1,0:T(8,128)(2,1)}) custom-call(s32[3]{0:T(128)} %pad_add_fusion.1.r_0_, bf16[1024,640]{1,0:T(8,128)(2,1)} %get-tuple-element.69.r_1_.r_2_, bf16[1024,512]{1,0:T(8,128)(2,1)} %get-tuple-element.64.r_6_.r_2_, bf16[1024,256]{1,0:T(8,128)(2,1)} %get-tuple-element.70.r_3_, ...), custom_call_target="tpu_custom_call" | custom-call | flops 4000000000 | bytes 1048576 | tf_op jit(solution)/shard_map/pallas_call | solution.py:652
  145.8 17.1 %collective-permute-done.29 = bf16[256,512]{1,0:T(8,128)(2,1)S(1)} collective-permute-done((bf16[256,512]{1,0:T(8,128)(2,1)S(1)}, bf16[256,512]{1,0:T(8,128)(2,1)S(1)}, u32[]{:S(2)}, u32[]{:S(2)}) %collective-permute-start.29) | collective-permute-done | bytes 262176 | tf_op jit(solution)/shard_map/ppermute | solution.py:639
  166.3 7.8 %collective-permute-done.39 = bf16[256,256]{1,0:T(8,128)(2,1)S(1)} collective-permute-done((bf16[256,256]{1,0:T(8,128)(2,1)S(1)}, bf16[256,256]{1,0:T(8,128)(2,1)S(1)}, u32[]{:S(2)}, u32[]{:S(2)}) %collective-permute-start.39) | collective-permute-done | bytes 131104 | tf_op jit(solution)/shard_map/ppermute | solution.py:639
  180.4 3.8 %collective-permute-done.33.r_4_ = bf16[256,512]{1,0:T(8,128)(2,1)S(1)} collective-permute-done((bf16[256,512]{1,0:T(8,128)(2,1)S(1)}, bf16[256,512]{1,0:T(8,128)(2,1)S(1)}, u32[]{:S(2)}, u32[]{:S(2)}) %collective-permute-start.33) | collective-permute-done | bytes 262176 | tf_op jit(solution)/shard_map/ppermute | solution.py:639
  189.9 4.4 %collective-permute-done.43.r_8_ = bf16[256,512]{1,0:T(8,128)(2,1)S(1)} collective-permute-done((bf16[256,512]{1,0:T(8,128)(2,1)S(1)}, bf16[256,512]{1,0:T(8,128)(2,1)S(1)}, u32[]{:S(2)}, u32[]{:S(2)}) %collective-permute-start.43) | collective-permute-done | bytes 262176 | tf_op jit(solution)/shard_map/ppermute | solution.py:639
  195.0 3.9 %shard_map.277 = (f32[256,2,1024]{2,1,0:T(2,128)}, f32[16,256]{1,0:T(8,128)}, f32[1,256]{1,0:T(1,128)}, f32[4,16,16]{2,1,0:T(8,128)}, f32[16,16]{1,0:T(8,128)}, ...) custom-call(s32[3]{0:T(128)} %pad_add_fusion.1.r_0_, ...), custom_call_target="tpu_custom_call" | custom-call | flops 4000000000 | bytes 1048576 | tf_op jit(solution)/shard_map/pallas_call | solution.py:652
  205.6 3.1 %collective-permute-done.24 = bf16[256,512]{1,0:T(8,128)(2,1)S(1)} collective-permute-done((bf16[256,512]{1,0:T(8,128)(2,1)S(1)}, bf16[256,512]{1,0:T(8,128)(2,1)S(1)}, u32[]{:S(2)}, u32[]{:S(2)}) %collective-permute-start.24) | collective-permute-done | bytes 262176 | tf_op jit(solution)/shard_map/ppermute | solution.py:639
  210.2 3.8 %collective-permute-done.25 = bf16[256,512]{1,0:T(8,128)(2,1)S(1)} collective-permute-done((bf16[256,512]{1,0:T(8,128)(2,1)S(1)}, bf16[256,512]{1,0:T(8,128)(2,1)S(1)}, u32[]{:S(2)}, u32[]{:S(2)}) %collective-permute-start.25) | collective-permute-done | bytes 262176 | tf_op jit(solution)/shard_map/ppermute | solution.py:639
  216.3 3.7 %collective-permute-done.20 = bf16[256,512]{1,0:T(8,128)(2,1)S(1)} collective-permute-done((bf16[256,512]{1,0:T(8,128)(2,1)S(1)}, bf16[256,512]{1,0:T(8,128)(2,1)S(1)}, u32[]{:S(2)}, u32[]{:S(2)}) %collective-permute-start.20) | collective-permute-done | bytes 262176 | tf_op jit(solution)/shard_map/ppermute | solution.py:639
  219.9 5.6 %collective-permute-done.22 = bf16[256,512]{1,0:T(8,128)(2,1)S(1)} collective-permute-done((bf16[256,512]{1,0:T(8,128)(2,1)S(1)}, bf16[256,512]{1,0:T(8,128)(2,1)S(1)}, u32[]{:S(2)}, u32[]{:S(2)}) %collective-permute-start.22) | collective-permute-done | bytes 262176 | tf_op jit(solution)/shard_map/ppermute | solution.py:639
  (226 shorter events, 71.3 us)
Async XLA Ops:
  12.3 15.9 %collective-permute-start = (bf16[256,1024]{1,0:T(8,128)(2,1)S(1)}, bf16[256,1024]{1,0:T(8,128)(2,1)}, u32[]{:S(2)}, u32[]{:S(2)}) collective-permute-start(bf16[256,1024]{1,0:T(8,128)(2,1)S(1)} %pad_maximum_fusion), channel_id=1, source_target_pairs={{0,2},{2,0},{4,6},{6,4},{1,3},{3,1},{5,7},{7,5},{8,10},{10,8},{12,... | collective-permute-start | bytes 1572872 | tf_op jit(solution)/shard_map/ppermute | solution.py:639
  13.9 24.4 %collective-permute-start.1 = (bf16[256,1024]{1,0:T(8,128)(2,1)S(1)}, bf16[256,1024]{1,0:T(8,128)(2,1)}, u32[]{:S(2)}, u32[]{:S(2)}) collective-permute-start(bf16[256,1024]{1,0:T(8,128)(2,1)S(1)} %pad_maximum_fusion), channel_id=1, source_target_pairs={{0,4},{2,6},{4,0},{6,2},{1,5},{3,7},{5,1},{7,3},{8,12},{10,14},{12... | collective-permute-start | bytes 1572872 | tf_op jit(solution)/shard_map/ppermute | solution.py:639
  15.4 22.9 %collective-permute-start.2 = (bf16[256,1024]{1,0:T(8,128)(2,1)S(1)}, bf16[256,1024]{1,0:T(8,128)(2,1)}, u32[]{:S(2)}, u32[]{:S(2)}) collective-permute-start(bf16[256,1024]{1,0:T(8,128)(2,1)S(1)} %pad_maximum_fusion), channel_id=1, source_target_pairs={{0,6},{2,4},{4,2},{6,0},{1,7},{3,5},{5,3},{7,1},{8,14},{10,12},{12... | collective-permute-start | bytes 1572872 | tf_op jit(solution)/shard_map/ppermute | solution.py:639
  22.4 16.5 %collective-permute-start.6 = (bf16[256,256]{1,0:T(8,128)(2,1)S(1)}, bf16[256,256]{1,0:T(8,128)(2,1)S(1)}, u32[]{:S(2)}, u32[]{:S(2)}) collective-permute-start(bf16[256,256]{1,0:T(8,128)(2,1)S(1)} %bitcast.77), channel_id=1, source_target_pairs={{0,8},{8,0},{16,24},{24,16},{1,9},{9,1},{17,25},{25,17},{2,10},{10... | collective-permute-start | bytes 393224 | tf_op jit(solution)/shard_map/ppermute | solution.py:639
  25.3 13.7 %collective-permute-start.7 = (bf16[256,256]{1,0:T(8,128)(2,1)S(1)}, bf16[256,256]{1,0:T(8,128)(2,1)S(1)}, u32[]{:S(2)}, u32[]{:S(2)}) collective-permute-start(bf16[256,256]{1,0:T(8,128)(2,1)S(1)} %bitcast.78), channel_id=1, source_target_pairs={{0,16},{8,24},{16,0},{24,8},{1,17},{9,25},{17,1},{25,9},{2,18},{10... | collective-permute-start | bytes 393224 | tf_op jit(solution)/shard_map/ppermute | solution.py:639
  28.2 22.3 %collective-permute-start.3 = (bf16[256,1024]{1,0:T(8,128)(2,1)}, bf16[256,1024]{1,0:T(8,128)(2,1)S(1)}, u32[]{:S(2)}, u32[]{:S(2)}) collective-permute-start(bf16[256,1024]{1,0:T(8,128)(2,1)} %collective-permute-done.r_6_), channel_id=1, source_target_pairs={{0,1},{1,0},{2,3},{3,2},{4,5},{5,4},{6,7},{7,6},{8,9},{9,8},{10,11... | collective-permute-start | bytes 1572872 | tf_op jit(solution)/shard_map/ppermute | solution.py:639
  38.3 13.7 %collective-permute-start.4 = (bf16[256,1024]{1,0:T(8,128)(2,1)}, bf16[256,1024]{1,0:T(8,128)(2,1)}, u32[]{:S(2)}, u32[]{:S(2)}) collective-permute-start(bf16[256,1024]{1,0:T(8,128)(2,1)} %collective-permute-done.1.r_7_), channel_id=1, source_target_pairs={{0,1},{1,0},{2,3},{3,2},{4,5},{5,4},{6,7},{7,6},{8,9},{9,8},{10,11... | collective-permute-start | bytes 1572872 | tf_op jit(solution)/shard_map/ppermute | solution.py:639
  47.0 20.2 %collective-permute-start.13 = (bf16[256,512]{1,0:T(8,128)(2,1)S(1)}, bf16[256,512]{1,0:T(8,128)(2,1)S(1)}, u32[]{:S(2)}, u32[]{:S(2)}) collective-permute-start(bf16[256,512]{1,0:T(8,128)(2,1)S(1)} %pad_maximum_fusion.2.r_5_), channel_id=1, source_target_pairs={{0,8},{8,0},{16,24},{24,16},{1,9},{9,1},{17,25},{25,17},{2,10},{10... | collective-permute-start | bytes 786440 | tf_op jit(solution)/shard_map/ppermute | solution.py:639
  49.4 21.3 %collective-permute-start.14 = (bf16[256,512]{1,0:T(8,128)(2,1)S(1)}, bf16[256,512]{1,0:T(8,128)(2,1)S(1)}, u32[]{:S(2)}, u32[]{:S(2)}) collective-permute-start(bf16[256,512]{1,0:T(8,128)(2,1)S(1)} %pad_maximum_fusion.2.r_5_), channel_id=1, source_target_pairs={{0,16},{8,24},{16,0},{24,8},{1,17},{9,25},{17,1},{25,9},{2,18},{10... | collective-permute-start | bytes 786440 | tf_op jit(solution)/shard_map/ppermute | solution.py:639
  50.5 20.2 %collective-permute-start.15 = (bf16[256,512]{1,0:T(8,128)(2,1)S(1)}, bf16[256,512]{1,0:T(8,128)(2,1)S(1)}, u32[]{:S(2)}, u32[]{:S(2)}) collective-permute-start(bf16[256,512]{1,0:T(8,128)(2,1)S(1)} %pad_maximum_fusion.2.r_5_), channel_id=1, source_target_pairs={{0,24},{8,16},{16,8},{24,0},{1,25},{9,17},{17,9},{25,1},{2,26},{10... | collective-permute-start | bytes 786440 | tf_op jit(solution)/shard_map/ppermute | solution.py:639
  96.4 47.5 %collective-permute-start.28 = (bf16[256,512]{1,0:T(8,128)(2,1)}, bf16[256,512]{1,0:T(8,128)(2,1)S(1)}, u32[]{:S(2)}, u32[]{:S(2)}) collective-permute-start(bf16[256,512]{1,0:T(8,128)(2,1)} %get-tuple-element.80), channel_id=1, source_target_pairs={{0,8},{8,0},{16,24},{24,16},{1,9},{9,1},{17,25},{25,17},{2,10},{10... | collective-permute-start | bytes 786440 | tf_op jit(solution)/shard_map/ppermute | solution.py:639
  138.9 23.9 %collective-permute-start.29 = (bf16[256,512]{1,0:T(8,128)(2,1)S(1)}, bf16[256,512]{1,0:T(8,128)(2,1)S(1)}, u32[]{:S(2)}, u32[]{:S(2)}) collective-permute-start(bf16[256,512]{1,0:T(8,128)(2,1)S(1)} %copy-done.27), channel_id=1, source_target_pairs={{0,16},{8,24},{16,0},{24,8},{1,17},{9,25},{17,1},{25,9},{2,18},{10... | collective-permute-start | bytes 786440 | tf_op jit(solution)/shard_map/ppermute | solution.py:639
  140.1 24.0 %collective-permute-start.30 = (bf16[256,512]{1,0:T(8,128)(2,1)S(1)}, bf16[256,512]{1,0:T(8,128)(2,1)S(1)}, u32[]{:S(2)}, u32[]{:S(2)}) collective-permute-start(bf16[256,512]{1,0:T(8,128)(2,1)S(1)} %copy-done.26), channel_id=1, source_target_pairs={{0,24},{8,16},{16,8},{24,0},{1,25},{9,17},{17,9},{25,1},{2,26},{10... | collective-permute-start | bytes 786440 | tf_op jit(solution)/shard_map/ppermute | solution.py:639
  142.5 56.4 %collective-permute-start.23 = (bf16[1024,512]{1,0:T(8,128)(2,1)}, bf16[1024,512]{1,0:T(8,128)(2,1)S(1)}, u32[]{:S(2)}, u32[]{:S(2)}) collective-permute-start(bf16[1024,512]{1,0:T(8,128)(2,1)} %get-tuple-element.78), channel_id=1, source_target_pairs={{0,1},{1,0},{2,3},{3,2},{4,5},{5,4},{6,7},{7,6},{8,9},{9,8},{10,11... | collective-permute-start | bytes 3145736 | tf_op jit(solution)/shard_map/ppermute | solution.py:639
  143.7 21.2 %collective-permute-start.38 = (bf16[256,256]{1,0:T(8,128)(2,1)S(1)}, bf16[256,256]{1,0:T(8,128)(2,1)S(1)}, u32[]{:S(2)}, u32[]{:S(2)}) collective-permute-start(bf16[256,256]{1,0:T(8,128)(2,1)S(1)} %get-tuple-element.113), channel_id=1, source_target_pairs={{0,8},{8,0},{16,24},{24,16},{1,9},{9,1},{17,25},{25,17},{2,10},{10... | collective-permute-start | bytes 393224 | tf_op jit(solution)/shard_map/ppermute | solution.py:639
  143.9 30.2 %collective-permute-start.39 = (bf16[256,256]{1,0:T(8,128)(2,1)S(1)}, bf16[256,256]{1,0:T(8,128)(2,1)S(1)}, u32[]{:S(2)}, u32[]{:S(2)}) collective-permute-start(bf16[256,256]{1,0:T(8,128)(2,1)S(1)} %get-tuple-element.115), channel_id=1, source_target_pairs={{0,16},{8,24},{16,0},{24,8},{1,17},{9,25},{17,1},{25,9},{2,18},{10... | collective-permute-start | bytes 393224 | tf_op jit(solution)/shard_map/ppermute | solution.py:639
  175.7 14.2 %collective-permute-start.41 = (bf16[256,512]{1,0:T(8,128)(2,1)S(1)}, bf16[256,512]{1,0:T(8,128)(2,1)S(1)}, u32[]{:S(2)}, u32[]{:S(2)}) collective-permute-start(bf16[256,512]{1,0:T(8,128)(2,1)S(1)} %pad_maximum_fusion.3.r_5_), channel_id=1, source_target_pairs={{0,2},{2,0},{4,6},{6,4},{1,3},{3,1},{5,7},{7,5},{8,10},{10,8},{12,... | collective-permute-start | bytes 786440 | tf_op jit(solution)/shard_map/ppermute | solution.py:639
  177.8 16.5 %collective-permute-start.43 = (bf16[256,512]{1,0:T(8,128)(2,1)S(1)}, bf16[256,512]{1,0:T(8,128)(2,1)S(1)}, u32[]{:S(2)}, u32[]{:S(2)}) collective-permute-start(bf16[256,512]{1,0:T(8,128)(2,1)S(1)} %pad_maximum_fusion.3.r_5_), channel_id=1, source_target_pairs={{0,6},{2,4},{4,2},{6,0},{1,7},{3,5},{5,3},{7,1},{8,14},{10,12},{12... | collective-permute-start | bytes 786440 | tf_op jit(solution)/shard_map/ppermute | solution.py:639
  184.2 18.8 %collective-permute-start.19 = (bf16[1024,512]{1,0:T(8,128)(2,1)S(1)}, bf16[1024,512]{1,0:T(8,128)(2,1)S(1)}, u32[]{:S(2)}, u32[]{:S(2)}) collective-permute-start(bf16[1024,512]{1,0:T(8,128)(2,1)S(1)} %copy-done.24), channel_id=1, source_target_pairs={{0,1},{1,0},{2,3},{3,2},{4,5},{5,4},{6,7},{7,6},{8,9},{9,8},{10,11... | collective-permute-start | bytes 3145736 | tf_op jit(solution)/shard_map/ppermute | solution.py:639
  199.8 14.1 %collective-permute-start.25 = (bf16[256,512]{1,0:T(8,128)(2,1)S(1)}, bf16[256,512]{1,0:T(8,128)(2,1)S(1)}, u32[]{:S(2)}, u32[]{:S(2)}) collective-permute-start(bf16[256,512]{1,0:T(8,128)(2,1)S(1)} %get-tuple-element.107), channel_id=1, source_target_pairs={{0,4},{2,6},{4,0},{6,2},{1,5},{3,7},{5,1},{7,3},{8,12},{10,14},{12... | collective-permute-start | bytes 786440 | tf_op jit(solution)/shard_map/ppermute | solution.py:639
  201.5 13.7 %collective-permute-start.26 = (bf16[256,512]{1,0:T(8,128)(2,1)S(1)}, bf16[256,512]{1,0:T(8,128)(2,1)S(1)}, u32[]{:S(2)}, u32[]{:S(2)}) collective-permute-start(bf16[256,512]{1,0:T(8,128)(2,1)S(1)} %get-tuple-element.106), channel_id=1, source_target_pairs={{0,6},{2,4},{4,2},{6,0},{1,7},{3,5},{5,3},{7,1},{8,14},{10,12},{12... | collective-permute-start | bytes 786440 | tf_op jit(solution)/shard_map/ppermute | solution.py:639
  203.4 16.5 %collective-permute-start.20 = (bf16[256,512]{1,0:T(8,128)(2,1)S(1)}, bf16[256,512]{1,0:T(8,128)(2,1)S(1)}, u32[]{:S(2)}, u32[]{:S(2)}) collective-permute-start(bf16[256,512]{1,0:T(8,128)(2,1)S(1)} %get-tuple-element.108), channel_id=1, source_target_pairs={{0,2},{2,0},{4,6},{6,4},{1,3},{3,1},{5,7},{7,5},{8,10},{10,8},{12,... | collective-permute-start | bytes 786440 | tf_op jit(solution)/shard_map/ppermute | solution.py:639
  203.8 16.1 %collective-permute-start.21 = (bf16[256,512]{1,0:T(8,128)(2,1)S(1)}, bf16[256,512]{1,0:T(8,128)(2,1)S(1)}, u32[]{:S(2)}, u32[]{:S(2)}) collective-permute-start(bf16[256,512]{1,0:T(8,128)(2,1)S(1)} %get-tuple-element.110), channel_id=1, source_target_pairs={{0,4},{2,6},{4,0},{6,2},{1,5},{3,7},{5,1},{7,3},{8,12},{10,14},{12... | collective-permute-start | bytes 786440 | tf_op jit(solution)/shard_map/ppermute | solution.py:639
  208.7 16.8 %collective-permute-start.22 = (bf16[256,512]{1,0:T(8,128)(2,1)S(1)}, bf16[256,512]{1,0:T(8,128)(2,1)S(1)}, u32[]{:S(2)}, u32[]{:S(2)}) collective-permute-start(bf16[256,512]{1,0:T(8,128)(2,1)S(1)} %get-tuple-element.109), channel_id=1, source_target_pairs={{0,6},{2,4},{4,2},{6,0},{1,7},{3,5},{5,3},{7,1},{8,14},{10,12},{12... | collective-permute-start | bytes 786440 | tf_op jit(solution)/shard_map/ppermute | solution.py:639
  (59 other events, 678.9 us)
